TPU v7x, 32 devices: a whole 2x2x4 slice. The times are simulated.
32 devices in a mesh: dp: 8 (over y, x, core), mp: 4 (over z).
Axes of the slice: x: 2, y: 2, z: 4, core: 2. Of those that a mesh axis runs over, the one named last changes fastest.
Arguments:
- tokens: bfloat16 [2048, 8192], P('dp', 'mp'), may hold values from -8 to 8
- attn_gain: bfloat16 [8192], replicated, may hold values from 0.5 to 1.5
- w_query: bfloat16 [8192, 4096], P('dp', 'mp'), may hold values from -2 to 2
- key_projection_weight: bfloat16 [8192, 512], P('dp', 'mp'), may hold values from -2 to 2
- value_projection_weight: bfloat16 [8192, 512], P('dp', 'mp'), may hold values from -0.0625 to 0.0625
- w_out: bfloat16 [4096, 8192], P('mp', 'dp'), may hold values from -0.09375 to 0.09375
- final_gain: bfloat16 [8192], P('mp'), may hold values from 0.5 to 1.5
- unembed: bfloat16 [64128, 8192], P('dp', 'mp'), may hold values from -0.29882812 to 0.29882812
- clean_ids: int32 [8], replicated, may hold values from 0 to 64127, as said below
- corrupt_ids: int32 [8], replicated, may hold values from 0 to 64127
Outputs:
- head_out: bfloat16 [2048, 4096], P('dp', 'mp')
- scores: float32 [8, 32], P('dp', 'mp')
- metric: float32 [8], P('dp')
Inputs may be any that keep to these rules, and one draw needn't show every extreme that they name: `clean_ids`: split the ids into 8 aligned blocks of equal size and number the groups of 1 sequence alike; the block of a clean answer, minus the number of its sequence's group, taken modulo the number of blocks, is drawn so that every such offset occurs for some sequence.
All inputs are finite; a program needn't handle non-finite values.
Results may differ from a plain program's by a relative error of at most 0.015.
Values may be sent and summed in bfloat16 or wider, within the bound.
A program may use at most 128 MiB of HBM per device.

v0:
```python
import functools
import math

import jax
import jax.numpy as jnp
import numpy as np
from jax import lax
from jax.experimental import pallas as pl
from jax.experimental.pallas import tpu as pltpu
from jax.sharding import PartitionSpec as P

HEAD_SIZE = 128
SEQUENCE_LENGTH = 256
MESH = pl.DeviceIdType.MESH
F32 = jnp.float32
BF16 = jnp.bfloat16


def flip(index, mask):
    bit = 1
    out = index
    while bit <= mask:
        if mask & bit:
            out = out + bit - 2 * bit * ((index // bit) % 2)
        bit *= 2
    return out


def spread_plan(size):
    bits = []
    bit = 2
    while bit < size:
        bits.append(bit)
        bit *= 2
    parts = min(2, len(bits))
    plan = []
    for part in range(parts):
        order = bits[part:] + bits[:part]
        held = [0]
        arrivals = []
        for step, b in enumerate(order):
            fresh = [h ^ b for h in held]
            arrivals += [(f, step) for f in fresh]
            held = held + fresh
        plan.append((order, arrivals))
    return plan


def whole_kernel(
    D, M, chunks, xchunks, token_count,
    tok_ref, gain_ref, wq_ref, wk_ref, wv_ref, cos_hbm, sin_hbm, wout_hbm, contrib_ref, fgain_ref,
    head_ref, scores_ref, metric_ref,
    x_all, w_all, acc, cos_ref, sin_ref, wout_ref, tail_tok, q_s, k_s, v_s, tot_src,
    last_src, tot_all, last_all, rows_a, out_src, out_all, dir_all, sq_src, sq_all,
    g_src, g_all, hg_src, hg_all, rows_g,
    loc_sem, one_sem, xs_sem, xr_sem, ps_sem, pr_sem, cs_sem, cr_sem,
    s1, r1, s2, r2, s3, r3, s4, r4, s5, r5, s6, r6, s7, r7,
):
    d = lax.axis_index("dp")
    m = lax.axis_index("mp")
    plan = spread_plan(D)
    parts = len(plan)
    depth = wq_ref.shape[0]
    rows, width = tok_ref.shape
    qw, kw, vw = wq_ref.shape[1], wk_ref.shape[1], wv_ref.shape[1]
    piece = depth // (parts * chunks)
    xpiece = rows // xchunks
    L = SEQUENCE_LENGTH
    S = rows // L
    heads, kv_heads = qw // HEAD_SIZE, kw // HEAD_SIZE
    G = heads // kv_heads
    cols = wout_ref.shape[1]
    R = D // M
    everyone = D * M
    me = d * M + m
    model_width = M * width

    def wrows(p, c):
        return pl.ds((p * chunks + c) * piece, piece)

    own = []
    for c in range(chunks):
        for p in range(parts):
            rr = wrows(p, c)
            trio = []
            for i, (src, lo, n) in enumerate(
                ((wq_ref, 0, qw), (wk_ref, qw, kw), (wv_ref, qw + kw, vw))
            ):
                cp = pltpu.make_async_copy(
                    src.at[rr, :], w_all.at[d, rr, pl.ds(lo, n)], loc_sem.at[p, c, i]
                )
                cp.start()
                trio.append(cp)
            own.append((p, c, trio))

    barrier = pltpu.get_barrier_semaphore()

    @pl.loop(1, everyone)
    def _(i):
        other = (me + i) % everyone
        pl.semaphore_signal(
            barrier, inc=1, device_id=(other // M, other % M), device_id_type=MESH
        )

    xown = pltpu.make_async_copy(tok_ref, x_all.at[m], one_sem.at[0])
    early = [
        pltpu.make_async_copy(cos_hbm, cos_ref, one_sem.at[1]),
        pltpu.make_async_copy(sin_hbm, sin_ref, one_sem.at[2]),
        pltpu.make_async_copy(wout_hbm, wout_ref, one_sem.at[3]),
    ]
    for b in range(S):
        early.append(pltpu.make_async_copy(
            tok_ref.at[pl.ds((b + 1) * L - 16, 16), :], tail_tok.at[b], one_sem.at[4 + b]
        ))
    pl.semaphore_wait(barrier, everyone - 1)

    pending = []

    def remote(src, dst, ss, rs, to, cond=None):
        cp = pltpu.make_async_remote_copy(
            src_ref=src, dst_ref=dst, send_sem=ss, recv_sem=rs, device_id=to, device_id_type=MESH
        )
        if cond is None:
            cp.start()
        else:
            pl.when(cond)(cp.start)
        pending.append((cp, cond))

    def local(src, dst, rs, cond=None):
        cp = pltpu.make_async_copy(src, dst, rs)
        if cond is None:
            cp.start()
        else:
            pl.when(cond)(cp.start)

    def arrive(buf, sem, n):
        for i in range(n):
            pltpu.make_async_copy(buf.at[i], buf.at[i], sem.at[i]).wait()

    def xsend(hop, c, side):
        rr = pl.ds(c * xpiece, xpiece)
        owner = m - hop if side == 0 else m + hop
        to = m + 1 if side == 0 else m - 1
        return pltpu.make_async_remote_copy(
            src_ref=(tok_ref.at[rr, :] if hop == 0 else x_all.at[owner, rr, :]),
            dst_ref=x_all.at[owner, rr, :],
            send_sem=xs_sem.at[hop, c, side],
            recv_sem=xr_sem.at[hop, c, side],
            device_id=(d, to),
            device_id_type=MESH,
        )

    def xpred(hop, side):
        if side == 0:
            return (m < M - 1) & (m - hop >= 0)
        return (m > 0) & (m + hop < M)

    def xstart(hop, c):
        for side in range(2):
            @pl.when(xpred(hop, side))
            def _(side=side):
                xsend(hop, c, side).start()

    def xwait(hop, c):
        rr = pl.ds(c * xpiece, xpiece)
        for side in range(2):
            owner = m - hop - 1 if side == 0 else m + hop + 1
            ok = (m - hop - 1 >= 0) if side == 0 else (m + hop + 1 < M)

            @pl.when(ok)
            def _(side=side, owner=owner):
                pltpu.make_async_copy(
                    x_all.at[owner, rr, :], x_all.at[owner, rr, :], xr_sem.at[hop, c, side]
                ).wait()

    def wcopy(mask, p, c, bit, send_sem, recv_sem):
        owner = flip(d, mask)
        rr = wrows(p, c)
        remote(w_all.at[owner, rr, :], w_all.at[owner, rr, :], send_sem, recv_sem,
               (flip(d, bit), m))

    def wsend(mask, p, c, step):
        bit = plan[p][0][step]
        wcopy(mask, p, c, bit, ps_sem.at[p, mask // 2, c, step],
              pr_sem.at[p, (mask ^ bit) // 2, c])

    def csend(mask, p, c):
        wcopy(mask, p, c, 1, cs_sem.at[p, mask // 2, c], cr_sem.at[p, mask // 2, c])

    def wwait(mask, p, c, sem):
        owner = flip(d, mask)
        rr = wrows(p, c)
        pltpu.make_async_copy(w_all.at[owner, rr, :], w_all.at[owner, rr, :], sem).wait()

    steps = len(plan[0][0])
    for i, (p, c, trio) in enumerate(own):
        for cp in trio:
            cp.wait()
        wsend(0, p, c, 0)
        if i == parts - 1:
            for cc in range(xchunks):
                xstart(0, cc)
    for step in range(1, steps):
        for c in range(chunks):
            for p in range(parts):
                wsend(0, p, c, step)
    for c in range(chunks):
        for p in range(parts):
            csend(0, p, c)
    xown.start()
    for cp in early:
        cp.start()
    for i in range(1, D):
        to = (d + i) % D
        remote(contrib_ref.at[to], dir_all.at[d], s2.at[i], r2.at[d], (to, m))
    local(contrib_ref.at[d], dir_all.at[d], r2.at[d])

    rounds = len(plan[0][1])
    wevents = [(r, c) for r in range(rounds) for c in range(chunks)]
    xevents = [(h, c) for h in range(M - 1) for c in range(xchunks)]
    merged = sorted(
        [((i + 1) / len(wevents), 1, e) for i, e in enumerate(wevents)]
        + [(0.8 * (i + 1) / len(xevents), 0, e) for i, e in enumerate(xevents)]
    )

    def use(owner, lo, n):
        base = owner * depth
        shard = base // width
        col = pl.multiple_of(base % width + lo, 128 if n % 128 == 0 else n)
        acc[...] += jnp.dot(
            x_all[shard, :, pl.ds(col, n)], w_all[owner, pl.ds(lo, n), :],
            preferred_element_type=F32,
        )

    every_piece = {(p, c) for p in range(parts) for c in range(chunks)}
    got = {0: set(every_piece)}
    used = set()
    late = []
    todo = []

    def sweep(left):
        whole = [k for k in got if got[k] == every_piece and not any((k, q) in used for q in every_piece)]
        for mask in whole:
            todo.append((mask, False))
            used.update((mask, q) for q in every_piece)
        todo.extend((mask, True) for mask in whole)
        fresh = sorted((k, q) for k in got for q in got[k] if (k, q) not in used)
        if piece % 128:
            fresh = []
        for mask, (p, c) in fresh:
            used.add((mask, (p, c)))
            use(flip(d, mask), (p * chunks + c) * piece, piece)
        finish()
        late.extend(fresh)
        drain(-(-len(todo) // max(1, left - 1)))

    def drain(n):
        for mask, paired in todo[:n]:
            if paired:
                for p, c in sorted(every_piece):
                    wwait(mask + 1, p, c, cr_sem.at[p, mask // 2, c])
            use(flip(d, mask + int(paired)), 0, depth)
        del todo[:n]

    def finish():
        for mask, (p, c) in late:
            wwait(mask + 1, p, c, cr_sem.at[p, mask // 2, c])
            use(flip(d, mask + 1), (p * chunks + c) * piece, piece)
        late.clear()

    x_left = len(xevents)
    for _, kind, (a, c) in merged:
        if kind == 0:
            xwait(a, c)
            if a + 1 < M - 1:
                xstart(a + 1, c)
            x_left -= 1
            if x_left == 0:
                xown.wait()
                total = jnp.zeros((rows, 1), F32)
                for k in range(M):
                    xv = x_all[k].astype(F32)
                    total = total + jnp.sum(xv * xv, axis=1, keepdims=True)
                inv = lax.rsqrt(total / model_width + 1e-05)
                for h in range(M - 1):
                    for cc in range(xchunks):
                        for side in range(2):
                            @pl.when(xpred(h, side))
                            def _(h=h, cc=cc, side=side):
                                xsend(h, cc, side).wait_send()
                for k in range(M):
                    g = gain_ref[k * width:(k + 1) * width].astype(F32).reshape(1, width)
                    x_all[k] = (x_all[k].astype(F32) * inv * g).astype(BF16)
                acc[...] = jnp.zeros_like(acc)
        else:
            for p in range(parts):
                mask, step = plan[p][1][a]
                wwait(mask, p, c, pr_sem.at[p, mask // 2, c])
                for later in range(step + 1, steps):
                    wsend(mask, p, c, later)
                csend(mask, p, c)
                got.setdefault(mask, set()).add((p, c))
            if x_left == 0:
                sweep(len(wevents) - wevents.index((a, c)))
    drain(len(todo))
    finish()

    for cp in early:
        cp.wait()
    half = HEAD_SIZE // 2

    def rope(x, cos, sin):
        turned = jnp.concatenate([x[:, half:], x[:, :half]], axis=1)
        return (x * cos + turned * sin).astype(BF16)

    def softmax(logits):
        e = jnp.exp(logits - jnp.max(logits, axis=1, keepdims=True))
        return (e / jnp.sum(e, axis=1, keepdims=True)).astype(BF16)

    def scaled(q, k):
        return lax.dot_general(
            q, k, (((1,), (1,)), ((), ())), preferred_element_type=F32
        ) / math.sqrt(HEAD_SIZE)

    for b in range(S):
        span_b = slice(b * L, (b + 1) * L)
        at_last = (b + 1) * L - 1
        for n in range(kv_heads):
            lo = qw + n * HEAD_SIZE
            k = rope(acc[span_b, lo:lo + HEAD_SIZE], cos_ref[...], sin_ref[...])
            v = acc[span_b, lo + kw:lo + kw + HEAD_SIZE].astype(BF16)
            k_s[b * kv_heads + n] = k
            v_s[b * kv_heads + n] = v
            for g in range(G):
                h = n * G + g
                q_s[g:g + 1, :] = acc[at_last:at_last + 1, h * HEAD_SIZE:(h + 1) * HEAD_SIZE]
            q = rope(q_s[...], cos_ref[L - 1:L, :], sin_ref[L - 1:L, :])
            mixed = jnp.dot(softmax(scaled(q, k)), v, preferred_element_type=F32)
            mixed = mixed.astype(BF16).astype(F32)
            for g in range(G):
                h = n * G + g
                last_src[b:b + 1, h * HEAD_SIZE:(h + 1) * HEAD_SIZE] = mixed[g:g + 1, :]
    for i in range(1, D):
        to = (d + i) % D
        remote(last_src, last_all.at[d], s1.at[i], r1.at[d], (to, m))
    local(last_src, last_all.at[d], r1.at[d])

    ahead = lax.broadcasted_iota(jnp.int32, (L, L), 0) >= lax.broadcasted_iota(jnp.int32, (L, L), 1)

    def attend(first, end):
        for b in range(S):
            @pl.loop(first, end)
            def _(h):
                at = pl.ds(pl.multiple_of(h * HEAD_SIZE, HEAD_SIZE), HEAD_SIZE)
                n = b * kv_heads + h // G
                q = rope(acc[pl.ds(b * L, L), at], cos_ref[...], sin_ref[...])
                logits = jnp.where(ahead, scaled(q, k_s[n]), -1e30)
                mixed = jnp.dot(softmax(logits), v_s[n], preferred_element_type=F32).astype(BF16)
                head_ref[pl.ds(b * L, L), at] = mixed
                column = jnp.sum(mixed.astype(F32), axis=0, keepdims=True)
                if b == 0:
                    tot_src[:, at] = column
                else:
                    tot_src[:, at] += column

    cut = heads * 3 // 8
    attend(0, cut)
    arrive(last_all, r1, D)
    for j in range(D):
        rows_a[j * S:(j + 1) * S, 0:qw] = last_all[j]
    w = wout_ref[...]
    partial = jnp.dot(rows_a[:, 0:qw].astype(BF16), w, preferred_element_type=F32)
    for j in range(D):
        out_src[j] = partial[j * S:(j + 1) * S, :]
    span = d // R
    slot = (d % R) * M + m
    for i in range(D):
        to = (d + i) % D
        if i == 0:
            remote(out_src.at[to], out_all.at[slot], s3.at[i], r3.at[slot], (to, span), m != span)
            local(out_src.at[to], out_all.at[slot], r3.at[slot], m == span)
        else:
            remote(out_src.at[to], out_all.at[slot], s3.at[i], r3.at[slot], (to, span))

    attend(cut, heads)
    for i in range(1, D):
        to = (d + i) % D
        remote(tot_src, tot_all.at[d], s4.at[i], r4.at[d], (to, m))
    local(tot_src, tot_all.at[d], r4.at[d])
    arrive(dir_all, r2, D)
    direction = dir_all[0]
    for j in range(1, D):
        direction = direction + dir_all[j]
    weighted = fgain_ref[...].astype(F32).reshape(1, width) * direction

    arrive(out_all, r3, D)
    pieces = []
    for jj in range(R):
        part_sum = out_all[jj * M]
        for k in range(1, M):
            part_sum = part_sum + out_all[jj * M + k]
        pieces.append(part_sum)
    attn_last = jnp.concatenate(pieces, axis=1).astype(BF16).astype(F32)
    toks = [tail_tok[b].astype(F32)[15:16, :] for b in range(S)]
    residual = (toks[0] if S == 1 else jnp.concatenate(toks, axis=0)) + attn_last
    sq_src[0] = jnp.broadcast_to(jnp.sum(residual * residual, axis=1, keepdims=True), (S, 128))
    sq_src[1] = jnp.broadcast_to(jnp.sum(residual * weighted, axis=1, keepdims=True), (S, 128))
    for i in range(1, M):
        to = (m + i) % M
        remote(sq_src, sq_all.at[m], s5.at[i], r5.at[m], (d, to))
    local(sq_src, sq_all.at[m], r5.at[m])
    for jj in range(R):
        g_src[jj, 0:S, :] = weighted[:, jj * cols:(jj + 1) * cols]
        g_src[jj, S:2 * S, :] = residual[:, jj * cols:(jj + 1) * cols]
    for i in range(M - 1, -1, -1):
        k = (m + i) % M
        for jj in range(R):
            to = m * R + jj
            if i == 0:
                remote(g_src.at[jj], g_all.at[d], s6.at[jj, i], r6.at[d], (to, k), to != d)
                local(g_src.at[jj], g_all.at[d], r6.at[d], to == d)
            else:
                remote(g_src.at[jj], g_all.at[d], s6.at[jj, i], r6.at[d], (to, k))
    arrive(sq_all, r5, M)
    square = sq_all[0, 0]
    product = sq_all[0, 1]
    for k in range(1, M):
        square = square + sq_all[k, 0]
        product = product + sq_all[k, 1]
    inverse = lax.rsqrt(square / model_width + 1e-05)
    metric = inverse * product
    metric_ref[...] = metric[:, 0:1]
    fall = (metric * inverse * inverse / model_width)[:, 0:1]
    arrive(tot_all, r4, D)
    mean = tot_all[0]
    for j in range(1, D):
        mean = mean + tot_all[j]
    mean = mean / token_count
    arrive(g_all, r6, D)
    for j in range(D):
        rows_g[2 * j * S:2 * (j + 1) * S, :] = g_all[j]
    exact = rows_g[...]
    coarse = exact.astype(BF16)
    fine = (exact - coarse.astype(F32)).astype(BF16)
    both = lax.dot_general(
        jnp.concatenate([coarse, fine], axis=0), w, (((1,), (1,)), ((), ())),
        preferred_element_type=F32,
    )
    hg = both[:2 * D * S] + both[2 * D * S:]
    for j in range(D):
        hg_src[j] = hg[2 * j * S:2 * (j + 1) * S, :]
    for i in range(1, D):
        to = (d + i) % D
        remote(hg_src.at[to], hg_all.at[d], s7.at[i], r7.at[d], (to, m))
    local(hg_src.at[d], hg_all.at[d], r7.at[d])
    arrive(hg_all, r7, D)
    joint = hg_all[0]
    for j in range(1, D):
        joint = joint + hg_all[j]
    grads = joint[0:S] * inverse[:, 0:1] - joint[S:2 * S] * fall
    gap = (mean - last_src[...]) * grads
    lane = lax.broadcasted_iota(jnp.int32, (S, heads), 1)
    scores = jnp.zeros((S, heads), F32)
    for h in range(heads):
        part = jnp.sum(gap[:, h * HEAD_SIZE:(h + 1) * HEAD_SIZE], axis=1, keepdims=True)
        scores = jnp.where(lane == h, part, scores)
    scores_ref[...] = scores
    for cp, cond in pending:
        if cond is None:
            cp.wait_send()
        else:
            pl.when(cond)(cp.wait_send)


def tables():
    half = HEAD_SIZE // 2
    inv_freq = np.exp(np.arange(half) * (-2.0 * math.log(500000.0) / HEAD_SIZE))
    angles = np.arange(SEQUENCE_LENGTH)[:, None] * inv_freq[None, :]
    c, s = np.cos(angles), np.sin(angles)
    cos = np.concatenate([c, c], axis=1).astype(np.float32)
    return cos, np.concatenate([-s, s], axis=1).astype(np.float32)


def whole(D, M, tokens, gain, wq, wk, wv, w_out, contrib, final_gain):
    rows, width = tokens.shape
    S = rows // SEQUENCE_LENGTH
    depth = wq.shape[0]
    entries, cols = w_out.shape
    total = wq.shape[1] + wk.shape[1] + wv.shape[1]
    heads, kv_heads = wq.shape[1] // HEAD_SIZE, wk.shape[1] // HEAD_SIZE
    parts = len(spread_plan(D))
    steps = len(spread_plan(D)[0][0])
    chunks = max(1, min(4, depth // (128 * parts)))
    xchunks = 2
    half = D // 2
    R = D // M
    cos, sin = tables()
    DMA = pltpu.SemaphoreType.DMA
    ANY = pl.BlockSpec(memory_space=pl.ANY)
    V = pl.BlockSpec(memory_space=pltpu.VMEM)

    def f(*shape):
        return pltpu.VMEM(shape, F32)

    def h(*shape):
        return pltpu.VMEM(shape, BF16)

    return pl.pallas_call(
        functools.partial(whole_kernel, D, M, chunks, xchunks, rows * D),
        name="whole",
        out_shape=[
            jax.ShapeDtypeStruct((rows, entries), BF16),
            jax.ShapeDtypeStruct((S, heads), F32),
            jax.ShapeDtypeStruct((S, 1), F32),
        ],
        in_specs=[ANY, V, ANY, ANY, ANY, ANY, ANY, ANY, ANY, V],
        out_specs=[V, V, V],
        scratch_shapes=[
            h(M, rows, width), h(D, depth, total), f(rows, total),
            f(SEQUENCE_LENGTH, HEAD_SIZE), f(SEQUENCE_LENGTH, HEAD_SIZE),
            h(entries, cols), h(S, 16, width), f(heads // kv_heads, HEAD_SIZE),
            h(S * kv_heads, SEQUENCE_LENGTH, HEAD_SIZE), h(S * kv_heads, SEQUENCE_LENGTH, HEAD_SIZE),
            f(1, entries), f(S, entries), f(D, 1, entries), f(D, S, entries),
            f(D * S, max(entries, cols)), f(D, S, cols), f(D, S, cols), f(D, S, width),
            f(2, S, 128), f(M, 2, S, 128), f(R, 2 * S, cols), f(D, 2 * S, cols),
            f(D, 2 * S, entries), f(D, 2 * S, entries), f(2 * D * S, cols),
            DMA((parts, chunks, 3)), DMA((4 + S,)),
            DMA((M - 1, xchunks, 2)), DMA((M - 1, xchunks, 2)),
            DMA((parts, half, chunks, steps)), DMA((parts, half, chunks)),
            DMA((parts, half, chunks)), DMA((parts, half, chunks)),
            DMA((D,)), DMA((D,)), DMA((D,)), DMA((D,)), DMA((D,)), DMA((D,)), DMA((D,)), DMA((D,)),
            DMA((M,)), DMA((M,)), DMA((R, M)), DMA((D,)), DMA((D,)), DMA((D,)),
        ],
        compiler_params=pltpu.CompilerParams(
            collective_id=0, has_side_effects=True, vmem_limit_bytes=56 * 1024 * 1024
        ),
    )(tokens, gain, wq, wk, wv, jnp.asarray(cos), jnp.asarray(sin), w_out, contrib,
      final_gain)


GROUP = 16


def pick_kernel(per, vocab_rows, clean_ref, corrupt_ref, *refs):
    blocks, out_ref = refs[:-1], refs[-1]
    step = pl.program_id(0)
    start = lax.axis_index("dp") * vocab_rows
    where = lax.broadcasted_iota(jnp.int32, (GROUP, 1), 0)
    for i in range(per):
        rows = []
        for side in range(2):
            at = (clean_ref, corrupt_ref)[side][step * per + i] - start
            block = blocks[side * per + i][...].astype(F32)
            hit = (where == at % GROUP) & (at >= 0) & (at < vocab_rows)
            rows.append(jnp.sum(jnp.where(hit, block, 0.0), axis=0, keepdims=True))
        out_ref[i] = rows[0] - rows[1]


def pick(unembed, clean_ids, corrupt_ids):
    vocab_rows, width = unembed.shape
    n = clean_ids.shape[0]
    per = min(8, n)

    def spec(side, i):
        def index(step, *ids):
            at = ids[side][step * per + i] - lax.axis_index("dp") * vocab_rows
            return jnp.clip(at, 0, vocab_rows - 1) // GROUP, 0
        return pl.BlockSpec((GROUP, width), index)

    return pl.pallas_call(
        functools.partial(pick_kernel, per, vocab_rows),
        name="pick",
        grid_spec=pltpu.PrefetchScalarGridSpec(
            num_scalar_prefetch=2,
            grid=(n // per,),
            in_specs=[spec(side, i) for side in range(2) for i in range(per)],
            out_specs=pl.BlockSpec((per, 1, width), lambda step, *ids: (step, 0, 0)),
        ),
        out_shape=jax.ShapeDtypeStruct((n, 1, width), F32),
    )(clean_ids, corrupt_ids, *([unembed] * (2 * per)))


def per_device(
    D, M, tokens, attn_gain, w_query, key_w, value_w, w_out, final_gain, unembed,
    clean_ids, corrupt_ids,
):
    S = tokens.shape[0] // SEQUENCE_LENGTH
    width = unembed.shape[1]
    contrib = pick(unembed, clean_ids, corrupt_ids).reshape(D, S, width)
    head_out, scores, metric = whole(
        D, M, tokens, attn_gain, w_query, key_w, value_w, w_out, contrib, final_gain
    )
    return head_out, scores, metric.reshape(S)


def solution(mesh):
    in_specs = (
        P("dp", "mp"), P(), P("dp", "mp"), P("dp", "mp"), P("dp", "mp"),
        P("mp", "dp"), P("mp"), P("dp", "mp"), P(), P(),
    )
    out_specs = (P("dp", "mp"), P("dp", "mp"), P("dp"))
    return jax.shard_map(
        functools.partial(per_device, mesh.shape["dp"], mesh.shape["mp"]),
        mesh=mesh, in_specs=in_specs, out_specs=out_specs, check_vma=False,
    )
```

profile of v0, /device:TPU:0, one launch (start us, length us, event | category | flops | bytes accessed | tf_op | source)
XLA Modules:
  0.0 126.5 jit_solution(11317653528322677618)
XLA Ops:
  0.6 3.5 %pick.1.contrib_ref = f32[8,1,2048]{2,1,0:T(1,128)} custom-call(s32[8]{0:T(128)} %clean_ref.1, s32[8]{0:T(128)} %corrupt_ref.1, bf16[8016,2048]{1,0:T(8,128)(2,1)} %refs_15_.1, bf16[8016,2048]{1,0:T(8,128)(2,1)} %refs_15_.1, bf16[8016,2048]{1,0:T(8,128)(2,1)} %refs_15_.1, bf16[8016,2048]{1,0:T(8,128)(2,1)} %refs_15_.1, bf16[8016,2048]{1,0:T(8,128)(2,1)} %refs_15_.1, ...), custom_call_target="tpu_custom_call" | custom-call | tf_op jit(solution)/shard_map/pick/pallas_call | solution.py:570
  4.1 117.7 %whole.1 = (bf16[256,1024]{1,0:T(8,128)(2,1)}, f32[1,8]{1,0:T(1,128)}, f32[1,1]{1,0:T(1,128)}) custom-call(bf16[256,2048]{1,0:T(8,128)(2,1)} %tok_ref.1, bf16[8192]{0:T(1024)(128)(2,1)} %gain_ref.1, bf16[1024,1024]{1,0:T(8,128)(2,1)} %wq_ref.1, bf16[1024,128]{1,0:T(8,128)(2,1)} %wk_ref.1, bf16[1024,128]{1,0:T(8,128)(2,1)} %wv_ref.1, ...), custom_call_target="tpu_custom_call" | custom-call | tf_op jit(solution)/shard_map/whole/pallas_call | solution.py:508
  121.8 1.9 %copy.18 = bf16[256,1024]{1,0:T(8,128)(2,1)} copy(bf16[256,1024]{1,0:T(8,128)(2,1)} %get-tuple-element.12) | data formatting | bytes 1048576
  123.6 1.1 copy.19
where the time goes:
time: 127 us
  Pallas kernels  121 us (95%)
  local copies, waits for them, and re-layouts  2.97 us (2%)
  between operations  2.41 us (2%)
    pallas_call x1, Pallas kernels, whole(): pl.pallas_call(functools.partial(whole_kernel, D, M, chunks, xchunks, row...  118 us
    pallas_call x1, Pallas kernels, pick(): pl.pallas_call(functools.partial(pick_kernel, per, vocab_rows), name='pic...  3.46 us
    unnamed x2, local copies, waits for them, and re-layouts  2.97 us

commit v1 on v0

v1 whole, which is shorter than its diff:
```python
import functools
import math

import jax
import jax.numpy as jnp
import numpy as np
from jax import lax
from jax.experimental import pallas as pl
from jax.experimental.pallas import tpu as pltpu
from jax.sharding import PartitionSpec as P

HEAD_SIZE = 128
SEQUENCE_LENGTH = 256
MESH = pl.DeviceIdType.MESH
F32 = jnp.float32
BF16 = jnp.bfloat16


def flip(index, mask):
    bit = 1
    out = index
    while bit <= mask:
        if mask & bit:
            out = out + bit - 2 * bit * ((index // bit) % 2)
        bit *= 2
    return out


def spread_plan(size):
    bits = []
    bit = 2
    while bit < size:
        bits.append(bit)
        bit *= 2
    parts = min(2, len(bits))
    plan = []
    for part in range(parts):
        order = bits[part:] + bits[:part]
        held = [0]
        arrivals = []
        for step, b in enumerate(order):
            fresh = [h ^ b for h in held]
            arrivals += [(f, step) for f in fresh]
            held = held + fresh
        plan.append((order, arrivals))
    return plan


def head_groups(heads, piece):
    if piece < 256 or heads < 4:
        return [heads]
    sizes = [2] * ((heads - 2) // 2)
    return sizes + [1] * (heads - sum(sizes))


def order_tasks(events, tasks):
    done = dict(events)
    left = dict(tasks)
    clock = 0.0
    out = []
    while left:
        ready = {
            name: max([0.0] + [done[dep] + lag for dep, lag in deps])
            for name, (deps, dur, rank, fn) in left.items()
            if all(dep in done for dep, lag in deps)
        }
        now = [name for name in ready if ready[name] <= clock]
        if not now:
            clock = min(ready.values())
            continue
        name = min(now, key=lambda n: (left[n][2], ready[n]))
        deps, dur, rank, fn = left.pop(name)
        out.append((clock, fn))
        clock += dur
        done[name] = clock
    return out


def whole_kernel(
    D, M, sizes, xchunks, token_count,
    tok_ref, gain_ref, wq_ref, wk_ref, wv_ref, cos_hbm, sin_hbm, wout_hbm, contrib_ref, fgain_ref,
    head_ref, scores_ref, metric_ref,
    *scratch,
):
    G_ = len(sizes) + 1
    w_bufs = scratch[:G_]
    (
        x_all, x_n, acc, gain_s, ss, cos_ref, sin_ref, wout_ref, tail_tok, q_s, k_s, v_s,
        dir_all, g_src, g_all, qp_src, qp_all, pre_w, pre_t, last_src, last_all, rows_a,
        out_src, out_all, hg_src, hg_all, tot_src, tot_all,
        loc_sem, one_sem, xs_sem, xr_sem, ps_sem, pr_sem, cs_sem, cr_sem,
        s1, r1, s2, r2, s3, r3, s4, r4, s6, r6, s7, r7, s8, r8,
    ) = scratch[G_:]
    d = lax.axis_index("dp")
    m = lax.axis_index("mp")
    plan = spread_plan(D)
    parts = len(plan)
    steps = len(plan[0][0])
    depth = wq_ref.shape[0]
    rows, width = tok_ref.shape
    qw, kw, vw = wq_ref.shape[1], wk_ref.shape[1], wv_ref.shape[1]
    piece = depth // parts
    xpiece = rows // xchunks
    L = SEQUENCE_LENGTH
    S = rows // L
    heads, kv_heads = qw // HEAD_SIZE, kw // HEAD_SIZE
    per_kv = heads // kv_heads
    cols = wout_ref.shape[1]
    R = D // M
    everyone = D * M
    me = d * M + m
    model_width = M * width
    home = d // R
    half = HEAD_SIZE // 2
    DS = D * S

    spans = [(qw, kw + vw)]
    head_span = [None]
    at = 0
    for n in sizes:
        spans.append((at * HEAD_SIZE, n * HEAD_SIZE))
        head_span.append((at, at + n))
        at += n
    ngroups = len(spans)

    def wref(owner, g, p):
        return w_bufs[g].at[owner // R, pl.ds((owner % R) * depth + p * piece, piece), :]

    own = {}
    for g in range(ngroups):
        for p in range(parts):
            rr = pl.ds(p * piece, piece)
            dst = wref(d, g, p)
            lo, n = spans[g]
            if g == 0:
                moves = [(wk_ref.at[rr, :], dst.at[:, pl.ds(0, kw)]),
                         (wv_ref.at[rr, :], dst.at[:, pl.ds(kw, vw)])]
            else:
                moves = [(wq_ref.at[rr, pl.ds(lo, n)], dst)]
            own[g, p] = [
                pltpu.make_async_copy(a, b, loc_sem.at[g, p, i]) for i, (a, b) in enumerate(moves)
            ]
            for cp in own[g, p]:
                cp.start()

    barrier = pltpu.get_barrier_semaphore()

    @pl.loop(1, everyone)
    def _(i):
        other = (me + i) % everyone
        pl.semaphore_signal(
            barrier, inc=1, device_id=(other // M, other % M), device_id_type=MESH
        )

    xown = pltpu.make_async_copy(tok_ref, x_all.at[m], one_sem.at[0])
    early = [
        pltpu.make_async_copy(cos_hbm, cos_ref, one_sem.at[1]),
        pltpu.make_async_copy(sin_hbm, sin_ref, one_sem.at[2]),
        pltpu.make_async_copy(wout_hbm, wout_ref, one_sem.at[3]),
    ]
    for b in range(S):
        early.append(pltpu.make_async_copy(
            tok_ref.at[pl.ds((b + 1) * L - 16, 16), :], tail_tok.at[b], one_sem.at[4 + b]
        ))
    xown.start()
    for cp in early:
        cp.start()
    for k in range(M):
        gain_s[k] = gain_ref[k * width:(k + 1) * width].astype(F32).reshape(1, width)
    ss[...] = jnp.zeros_like(ss)
    pl.semaphore_wait(barrier, everyone - 1)

    pending = []

    def remote(src, dst, send_sem, recv_sem, to, cond=None):
        cp = pltpu.make_async_remote_copy(
            src_ref=src, dst_ref=dst, send_sem=send_sem, recv_sem=recv_sem,
            device_id=to, device_id_type=MESH,
        )
        if cond is None:
            cp.start()
        else:
            pl.when(cond)(cp.start)
        pending.append((cp, cond))

    def local(src, dst, sem, cond=None):
        cp = pltpu.make_async_copy(src, dst, sem)
        if cond is None:
            cp.start()
        else:
            pl.when(cond)(cp.start)

    def arrive(buf, sem, n):
        for i in range(n):
            pltpu.make_async_copy(buf.at[i], buf.at[i], sem.at[i]).wait()

    def spread(src, dst, send_sem, recv_sem, same=False):
        for i in range(1, D):
            to = (d + i) % D
            remote(src if same else src.at[to], dst.at[d], send_sem.at[i], recv_sem.at[d], (to, m))
        local(src if same else src.at[d], dst.at[d], recv_sem.at[d])

    def xsend(hop, c, side):
        rr = pl.ds(c * xpiece, xpiece)
        owner = m - hop if side == 0 else m + hop
        to = m + 1 if side == 0 else m - 1
        return pltpu.make_async_remote_copy(
            src_ref=(tok_ref.at[rr, :] if hop == 0 else x_all.at[owner, rr, :]),
            dst_ref=x_all.at[owner, rr, :],
            send_sem=xs_sem.at[hop, c, side],
            recv_sem=xr_sem.at[hop, c, side],
            device_id=(d, to),
            device_id_type=MESH,
        )

    def xpred(hop, side):
        if side == 0:
            return (m < M - 1) & (m - hop >= 0)
        return (m > 0) & (m + hop < M)

    def xstart(hop, c):
        for side in range(2):
            @pl.when(xpred(hop, side))
            def _(side=side):
                xsend(hop, c, side).start()

    def xwait(hop, c):
        rr = pl.ds(c * xpiece, xpiece)
        for side in range(2):
            owner = m - hop - 1 if side == 0 else m + hop + 1
            ok = (m - hop - 1 >= 0) if side == 0 else (m + hop + 1 < M)

            @pl.when(ok)
            def _(side=side, owner=owner):
                pltpu.make_async_copy(
                    x_all.at[owner, rr, :], x_all.at[owner, rr, :], xr_sem.at[hop, c, side]
                ).wait()

    def wcopy(mask, g, p, bit, send_sem, recv_sem):
        ref = wref(flip(d, mask), g, p)
        remote(ref, ref, send_sem, recv_sem, (flip(d, bit), m))

    def wsend(mask, g, p, step):
        bit = plan[p][0][step]
        wcopy(mask, g, p, bit, ps_sem.at[p, mask // 2, g, step],
              pr_sem.at[p, (mask ^ bit) // 2, g])

    def csend(mask, g, p):
        wcopy(mask, g, p, 1, cs_sem.at[p, mask // 2, g], cr_sem.at[p, mask // 2, g])

    def wwait(mask, g, p, sem):
        ref = wref(flip(d, mask), g, p)
        pltpu.make_async_copy(ref, ref, sem).wait()

    def own_ready(g, p):
        for cp in own.pop((g, p), []):
            cp.wait()

    def own_sends(g):
        for p in range(parts):
            own_ready(g, p)
            wsend(0, g, p, 0)
        for step in range(1, steps):
            for p in range(parts):
                wsend(0, g, p, step)
        for p in range(parts):
            csend(0, g, p)

    pace = 46e3
    hops = len(plan[0][0])
    rounds = len(plan[0][1])
    shard_time = rows * width * 2 / pace
    group_time = [(D // 2 - 1) * depth * n * 2 / hops / pace for _, n in spans]
    share = hops / rounds
    own_at, rel_at = {}, {}
    clock = 0.0
    queue = [("own", 0)] + ([("own", 1)] if ngroups > 1 else [])
    for g in range(ngroups):
        queue.append(("rel", g))
        if g + 2 < ngroups:
            queue.append(("own", g + 2))
    for kind, g in queue:
        if kind == "own":
            own_at[g] = clock
            clock += group_time[g] * share
        else:
            clock += group_time[g] * (1 - share)
            rel_at[g] = clock

    timed = []
    events = {}
    for g in range(ngroups):
        for i in range(rounds):
            alone = [plan[p][1][i][0] & (plan[p][1][i][0] - 1) == 0 for p in range(parts)]
            if all(alone):
                when = own_at[g] + group_time[g] * (plan[0][1][i][1] + 1) / rounds
            else:
                lead = group_time[g] * (rounds - 1 - i) / rounds
                when = rel_at[g] - lead

            def arrival(g=g, i=i):
                for p in range(parts):
                    mask, step = plan[p][1][i]
                    wwait(mask, g, p, pr_sem.at[p, mask // 2, g])
                    for later in range(step + 1, steps):
                        wsend(mask, g, p, later)
                    csend(mask, g, p)
                if i == 0 and g + 2 < ngroups:
                    own_sends(g + 2)

            timed.append((when, 0, len(timed), arrival))
            events["w", g, i] = when
    for h in range(M - 1):
        for c in range(xchunks):
            when = (h + (c + 1) / xchunks) * shard_time

            def xarrival(h=h, c=c):
                xwait(h, c)
                if h + 1 < M - 1:
                    xstart(h + 1, c)

            timed.append((when, 1, len(timed), xarrival))
            events["x", h, c] = when
    xdone = (M - 1) * shard_time
    events["start"] = 0.0

    core_waited = set()

    def partner(g, masks):
        for mask in masks:
            for p in range(parts):
                if (g, mask, p) not in core_waited:
                    core_waited.add((g, mask, p))
                    wwait(mask + 1, g, p, cr_sem.at[p, mask // 2, g])

    begun = set()

    def unit(shard, g, masks):
        partner(g, masks)
        lo, n = spans[g]
        part = jnp.dot(x_n[shard], w_bufs[g][shard], preferred_element_type=F32)
        if g in begun:
            acc[:, lo:lo + n] += part
        else:
            acc[:, lo:lo + n] = part
            begun.add(g)

    evens = list(range(0, D, 2))

    def gained(r):
        if r == 0:
            xown.wait()
        shard = flip(m, r)
        block = 32

        @pl.loop(0, rows // block)
        def _(i):
            rr = pl.ds(pl.multiple_of(i * block, block), block)
            xv = x_all[shard, rr, :].astype(F32)
            ss[rr, :] += jnp.sum(xv * xv, axis=1, keepdims=True)
            x_n[shard, rr, :] = (xv * gain_s[shard]).astype(BF16)

    def inverse_rms():
        ss[...] = lax.rsqrt(ss[...] / model_width + 1e-05)

    def rope(x, cos, sin):
        turned = jnp.concatenate([x[:, half:], x[:, :half]], axis=1)
        return (x * cos + turned * sin).astype(BF16)

    def scores_of(q, k):
        return lax.dot_general(
            q, k, (((1,), (1,)), ((), ())), preferred_element_type=F32
        ) / math.sqrt(HEAD_SIZE)

    def softmax(logits):
        e = jnp.exp(logits - jnp.max(logits, axis=1, keepdims=True))
        return (e * (1.0 / jnp.sum(e, axis=1, keepdims=True))).astype(BF16)

    def first_exchange():
        for cp in early:
            cp.wait()
        arrive(dir_all, r2, D)
        direction = dir_all[0]
        for j in range(1, D):
            direction = direction + dir_all[j]
        weighted = fgain_ref[...].astype(F32).reshape(1, width) * direction
        toks = [tail_tok[b].astype(F32)[15:16, :] for b in range(S)]
        tok = toks[0] if S == 1 else jnp.concatenate(toks, axis=0)
        for jj in range(R):
            g_src[jj, 0:S, :] = weighted[:, jj * cols:(jj + 1) * cols]
            g_src[jj, S:2 * S, :] = tok[:, jj * cols:(jj + 1) * cols]
        for i in range(M - 1, -1, -1):
            k = (m + i) % M
            for jj in range(R):
                to = m * R + jj
                if i == 0:
                    remote(g_src.at[jj], g_all.at[d], s6.at[jj, i], r6.at[d], (to, k), to != d)
                    local(g_src.at[jj], g_all.at[d], r6.at[d], to == d)
                else:
                    remote(g_src.at[jj], g_all.at[d], s6.at[jj, i], r6.at[d], (to, k))

    def stacked(which):
        got = [g_all[j][which * S:(which + 1) * S, :] for j in range(D)]
        return jnp.concatenate(got, axis=0)

    def last_queries():
        arrive(g_all, r6, D)
        block = pl.ds(pl.multiple_of((d % R) * cols, cols), cols)
        lhs = (stacked(1) * gain_s[home, :, block]).astype(BF16)
        mine = pl.ds((d % R) * depth, depth)
        for g in range(1, ngroups):
            lo, n = spans[g]
            for p in range(parts):
                own_ready(g, p)
            part = jnp.dot(lhs, w_bufs[g][home, mine, :], preferred_element_type=F32)
            for j in range(D):
                qp_src[j, :, lo:lo + n] = part[j * S:(j + 1) * S, :]
        spread(qp_src, qp_all, s8, r8)

    def turned_back(x):
        return lax.dot_general(
            x, wout_ref[...], (((1,), (1,)), ((), ())), preferred_element_type=F32
        )

    def early_grads():
        exact = stacked(0)
        coarse = exact.astype(BF16)
        fine = (exact - coarse.astype(F32)).astype(BF16)
        pre = turned_back(jnp.concatenate([coarse, fine, stacked(1).astype(BF16)], axis=0))
        pre_w[...] = pre[:DS] + pre[DS:2 * DS]
        pre_t[...] = pre[2 * DS:]

    def keys_values():
        for b in range(S):
            sb = slice(b * L, (b + 1) * L)
            for n in range(kv_heads):
                lo = qw + n * HEAD_SIZE
                inv = ss[sb, :]
                k_s[b * kv_heads + n] = rope(acc[sb, lo:lo + HEAD_SIZE] * inv, cos_ref[...], sin_ref[...])
                v_s[b * kv_heads + n] = (acc[sb, lo + kw:lo + kw + HEAD_SIZE] * inv).astype(BF16)

    def last_position():
        arrive(qp_all, r8, D)
        q_sum = qp_all[0]
        for j in range(1, D):
            q_sum = q_sum + qp_all[j]
        for b in range(S):
            end = (b + 1) * L - 1
            inv = ss[end:end + 1, :]
            for n in range(kv_heads):
                for g in range(per_kv):
                    h = n * per_kv + g
                    q_s[g:g + 1, :] = q_sum[b:b + 1, h * HEAD_SIZE:(h + 1) * HEAD_SIZE] * inv
                q = rope(q_s[...], cos_ref[L - 1:L, :], sin_ref[L - 1:L, :])
                mixed = jnp.dot(
                    softmax(scores_of(q, k_s[b * kv_heads + n])), v_s[b * kv_heads + n],
                    preferred_element_type=F32,
                ).astype(BF16).astype(F32)
                for g in range(per_kv):
                    h = n * per_kv + g
                    last_src[b:b + 1, h * HEAD_SIZE:(h + 1) * HEAD_SIZE] = mixed[g:g + 1, :]
        spread(last_src, last_all, s1, r1, same=True)

    def project_out():
        arrive(last_all, r1, D)
        for j in range(D):
            rows_a[j * S:(j + 1) * S, :] = last_all[j]
        out_src[...] = jnp.dot(
            rows_a[...].astype(BF16), wout_ref[...], preferred_element_type=F32
        )
        for i in range(1, M):
            to = (m + i) % M
            remote(out_src, out_all.at[m], s3.at[i], r3.at[m], (d, to))
        local(out_src, out_all.at[m], r3.at[m])

    def residual_grads():
        arrive(out_all, r3, M)
        total = out_all[0]
        for k in range(1, M):
            total = total + out_all[k]
        attn = total.astype(BF16)
        residual = stacked(1) + attn.astype(F32)
        sq = jnp.sum(residual * residual, axis=1, keepdims=True)
        prod = jnp.sum(residual * stacked(0), axis=1, keepdims=True)
        back = turned_back(attn) + pre_t[...]
        entries = back.shape[1]
        sq = jnp.broadcast_to(sq, (DS, entries))
        prod = jnp.broadcast_to(prod, (DS, entries))
        ahead = pre_w[...]
        for j in range(D):
            sj = slice(j * S, (j + 1) * S)
            hg_src[j, 0:S, :] = ahead[sj]
            hg_src[j, S:2 * S, :] = back[sj]
            hg_src[j, 2 * S:3 * S, :] = sq[sj]
            hg_src[j, 3 * S:4 * S, :] = prod[sj]
        spread(hg_src, hg_all, s7, r7)

    bands = 2
    band = L // bands
    below = (lax.broadcasted_iota(jnp.int32, (band, band), 0)
             >= lax.broadcasted_iota(jnp.int32, (band, band), 1))

    def attend(h):
        at = slice(h * HEAD_SIZE, (h + 1) * HEAD_SIZE)
        for b in range(S):
            n = b * kv_heads + h // per_kv
            sb = slice(b * L, (b + 1) * L)
            q = rope(acc[sb, at] * ss[sb, :], cos_ref[...], sin_ref[...])
            column = None
            for i in range(bands):
                lo, hi = i * band, (i + 1) * band
                logits = scores_of(q[lo:hi], k_s[n, 0:hi, :])
                diag = jnp.where(below, logits[:, lo:hi], -1e30)
                logits = diag if i == 0 else jnp.concatenate([logits[:, :lo], diag], axis=1)
                mixed = jnp.dot(
                    softmax(logits), v_s[n, 0:hi, :], preferred_element_type=F32
                ).astype(BF16)
                head_ref[b * L + lo:b * L + hi, at] = mixed
                part = jnp.sum(mixed.astype(F32), axis=0, keepdims=True)
                column = part if column is None else column + part
            if b == 0:
                tot_src[:, at] = column
            else:
                tot_src[:, at] += column

    def totals():
        spread(tot_src, tot_all, s4, r4, same=True)

    def finish():
        arrive(hg_all, r7, D)
        joint = hg_all[0]
        for j in range(1, D):
            joint = joint + hg_all[j]
        inverse = lax.rsqrt(joint[2 * S:3 * S, :] / model_width + 1e-05)
        metric = inverse * joint[3 * S:4 * S, :]
        metric_ref[...] = metric[:, 0:1]
        fall = metric * inverse * inverse / model_width
        grads = joint[0:S] * inverse - joint[S:2 * S] * fall
        arrive(tot_all, r4, D)
        mean = tot_all[0]
        for j in range(1, D):
            mean = mean + tot_all[j]
        mean = mean / token_count
        gap = (mean - last_src[...]) * grads
        lane = lax.broadcasted_iota(jnp.int32, (S, heads), 1)
        scores = jnp.zeros((S, heads), F32)
        for h in range(heads):
            part = jnp.sum(gap[:, h * HEAD_SIZE:(h + 1) * HEAD_SIZE], axis=1, keepdims=True)
            scores = jnp.where(lane == h, part, scores)
        scores_ref[...] = scores

    tasks = {}
    for r in range(M):
        deps = [("start", 2.0)] if r == 0 else [(("x", r - 1, xchunks - 1), 0.1)]
        tasks["gain", r] = (deps, 1.0, 0, functools.partial(gained, r))
    gains = [(("gain", r), 0.0) for r in range(M)]
    tasks["inv"] = (gains, 0.1, 0, inverse_rms)
    unit_names = {g: [] for g in range(ngroups)}
    for g in range(ngroups):
        cost = 0.25 * spans[g][1] / 128
        late = rel_at[g] > xdone
        for r in range(M):
            if late:
                masks = [k for k in range(D) if k // R == r and k % 2 == 0]
                deps = gains + [
                    (("w", g, i), 1.6) for i in range(rounds)
                    if i == 0 or any(plan[p][1][i][0] in masks for p in range(parts))
                ]
                fn = functools.partial(lambda g, r, ms: unit(flip(home, r), g, ms), g, r, masks)
            else:
                deps = [(("gain", r), 0.0)] + [(("w", g, i), 1.6) for i in range(rounds)]
                fn = functools.partial(lambda g, r: unit(flip(m, r), g, evens), g, r)
            tasks["unit", g, r] = (deps, cost, 1 if g == 0 else 4, fn)
            unit_names[g].append((("unit", g, r), 0.0))
    tasks["kv"] = (unit_names[0] + [("inv", 0.0)], 1.0, 1, keys_values)
    tasks["E2"] = ([("start", 5.0)], 0.5, 2, first_exchange)
    tasks["E3"] = ([("E2", 26.0)], 1.0, 2, last_queries)
    tasks["pre"] = ([("E3", 0.0)], 1.0, 5, early_grads)
    tasks["last"] = ([("kv", 0.0), ("E3", 20.0)], 1.5, 1, last_position)
    tasks["T1"] = ([("last", 8.0)], 1.0, 1, project_out)
    tasks["T2"] = ([("T1", 4.0), ("pre", 0.0)], 1.5, 1, residual_grads)
    for g in range(1, ngroups):
        for h in range(*head_span[g]):
            tasks["att", h] = ([("kv", 0.0)] + unit_names[g], 1.2, 6, functools.partial(attend, h))
    tasks["tot"] = ([(("att", h), 0.0) for h in range(heads)], 0.1, 7, totals)
    tasks["fin"] = ([("tot", 0.0), ("T2", 0.0)], 0.1, 8, finish)

    spread(contrib_ref, dir_all, s2, r2)
    for c in range(xchunks):
        xstart(0, c)
    own_sends(0)
    if ngroups > 1:
        own_sends(1)
    ordered = order_tasks(events, tasks)
    timed += [(when, 2, len(timed) + i, fn) for i, (when, fn) in enumerate(ordered)]
    for _, _, _, fn in sorted(timed, key=lambda t: t[:3]):
        fn()
    for g in range(ngroups):
        partner(g, evens)
    for h in range(M - 1):
        for c in range(xchunks):
            for side in range(2):
                @pl.when(xpred(h, side))
                def _(h=h, c=c, side=side):
                    xsend(h, c, side).wait_send()
    for cp, cond in pending:
        if cond is None:
            cp.wait_send()
        else:
            pl.when(cond)(cp.wait_send)


def tables():
    half = HEAD_SIZE // 2
    inv_freq = np.exp(np.arange(half) * (-2.0 * math.log(500000.0) / HEAD_SIZE))
    angles = np.arange(SEQUENCE_LENGTH)[:, None] * inv_freq[None, :]
    c, s = np.cos(angles), np.sin(angles)
    cos = np.concatenate([c, c], axis=1).astype(np.float32)
    return cos, np.concatenate([-s, s], axis=1).astype(np.float32)


def whole(D, M, tokens, gain, wq, wk, wv, w_out, contrib, final_gain):
    rows, width = tokens.shape
    S = rows // SEQUENCE_LENGTH
    depth = wq.shape[0]
    entries, cols = w_out.shape
    kvw = wk.shape[1] + wv.shape[1]
    total = wq.shape[1] + kvw
    heads, kv_heads = wq.shape[1] // HEAD_SIZE, wk.shape[1] // HEAD_SIZE
    parts = len(spread_plan(D))
    steps = len(spread_plan(D)[0][0])
    sizes = head_groups(heads, depth // parts)
    ngroups = len(sizes) + 1
    xchunks = 2
    half = D // 2
    R = D // M
    cos, sin = tables()
    DMA = pltpu.SemaphoreType.DMA
    ANY = pl.BlockSpec(memory_space=pl.ANY)
    V = pl.BlockSpec(memory_space=pltpu.VMEM)

    def f(*shape):
        return pltpu.VMEM(shape, F32)

    def h(*shape):
        return pltpu.VMEM(shape, BF16)

    return pl.pallas_call(
        functools.partial(whole_kernel, D, M, sizes, xchunks, rows * D),
        name="whole",
        out_shape=[
            jax.ShapeDtypeStruct((rows, entries), BF16),
            jax.ShapeDtypeStruct((S, heads), F32),
            jax.ShapeDtypeStruct((S, 1), F32),
        ],
        in_specs=[ANY, V, ANY, ANY, ANY, ANY, ANY, ANY, V, V],
        out_specs=[V, V, V],
        scratch_shapes=[h(M, width, n) for n in [kvw] + [k * HEAD_SIZE for k in sizes]] + [
            h(M, rows, width), h(M, rows, width), f(rows, total), f(M, 1, width), f(rows, 1),
            f(SEQUENCE_LENGTH, HEAD_SIZE), f(SEQUENCE_LENGTH, HEAD_SIZE),
            h(entries, cols), h(S, 16, width), f(heads // kv_heads, HEAD_SIZE),
            h(S * kv_heads, SEQUENCE_LENGTH, HEAD_SIZE), h(S * kv_heads, SEQUENCE_LENGTH, HEAD_SIZE),
            f(D, S, width), f(R, 2 * S, cols), f(D, 2 * S, cols),
            f(D, S, entries), f(D, S, entries), f(D * S, entries), f(D * S, entries),
            f(S, entries), f(D, S, entries), f(D * S, entries),
            f(D * S, cols), f(M, D * S, cols), f(D, 4 * S, entries), f(D, 4 * S, entries),
            f(1, entries), f(D, 1, entries),
            DMA((ngroups, parts, 2)), DMA((4 + S,)),
            DMA((M - 1, xchunks, 2)), DMA((M - 1, xchunks, 2)),
            DMA((parts, half, ngroups, steps)), DMA((parts, half, ngroups)),
            DMA((parts, half, ngroups)), DMA((parts, half, ngroups)),
            DMA((D,)), DMA((D,)), DMA((D,)), DMA((D,)), DMA((M,)), DMA((M,)), DMA((D,)), DMA((D,)),
            DMA((R, M)), DMA((D,)), DMA((D,)), DMA((D,)), DMA((D,)), DMA((D,)),
        ],
        compiler_params=pltpu.CompilerParams(
            collective_id=0, has_side_effects=True, vmem_limit_bytes=56 * 1024 * 1024
        ),
    )(tokens, gain, wq, wk, wv, jnp.asarray(cos), jnp.asarray(sin), w_out, contrib,
      final_gain)


GROUP = 16


def pick_kernel(per, vocab_rows, clean_ref, corrupt_ref, *refs):
    blocks, out_ref = refs[:-1], refs[-1]
    step = pl.program_id(0)
    start = lax.axis_index("dp") * vocab_rows
    where = lax.broadcasted_iota(jnp.int32, (GROUP, 1), 0)
    for i in range(per):
        rows = []
        for side in range(2):
            at = (clean_ref, corrupt_ref)[side][step * per + i] - start
            block = blocks[side * per + i][...].astype(F32)
            hit = (where == at % GROUP) & (at >= 0) & (at < vocab_rows)
            rows.append(jnp.sum(jnp.where(hit, block, 0.0), axis=0, keepdims=True))
        out_ref[i] = rows[0] - rows[1]


def pick(unembed, clean_ids, corrupt_ids):
    vocab_rows, width = unembed.shape
    n = clean_ids.shape[0]
    per = min(8, n)

    def spec(side, i):
        def index(step, *ids):
            at = ids[side][step * per + i] - lax.axis_index("dp") * vocab_rows
            return jnp.clip(at, 0, vocab_rows - 1) // GROUP, 0
        return pl.BlockSpec((GROUP, width), index)

    return pl.pallas_call(
        functools.partial(pick_kernel, per, vocab_rows),
        name="pick",
        grid_spec=pltpu.PrefetchScalarGridSpec(
            num_scalar_prefetch=2,
            grid=(n // per,),
            in_specs=[spec(side, i) for side in range(2) for i in range(per)],
            out_specs=pl.BlockSpec((per, 1, width), lambda step, *ids: (step, 0, 0)),
        ),
        out_shape=jax.ShapeDtypeStruct((n, 1, width), F32),
    )(clean_ids, corrupt_ids, *([unembed] * (2 * per)))


def per_device(
    D, M, tokens, attn_gain, w_query, key_w, value_w, w_out, final_gain, unembed,
    clean_ids, corrupt_ids,
):
    S = tokens.shape[0] // SEQUENCE_LENGTH
    width = unembed.shape[1]
    contrib = pick(unembed, clean_ids, corrupt_ids).reshape(D, S, width)
    head_out, scores, metric = whole(
        D, M, tokens, attn_gain, w_query, key_w, value_w, w_out, contrib, final_gain
    )
    return head_out, scores, metric.reshape(S)


def solution(mesh):
    in_specs = (
        P("dp", "mp"), P(), P("dp", "mp"), P("dp", "mp"), P("dp", "mp"),
        P("mp", "dp"), P("mp"), P("dp", "mp"), P(), P(),
    )
    out_specs = (P("dp", "mp"), P("dp", "mp"), P("dp"))
    return jax.shard_map(
        functools.partial(per_device, mesh.shape["dp"], mesh.shape["mp"]),
        mesh=mesh, in_specs=in_specs, out_specs=out_specs, check_vma=False,
    )
```

time: 127 us -> 118 us (0.929)
  Pallas kernels: 121 us -> 112 us
    pallas_call x1, Pallas kernels: 118 us -> 108 us  [whole(): pl.pallas_call(functools.partial(whole_kernel, D, M, sizes, xchunks, rows...]
where the time goes in v1:
time: 118 us; the launch traced here: 117 us
  Pallas kernels  112 us (95%)
  local copies, waits for them, and re-layouts  2.97 us (3%)
  between operations  2.41 us (2%)
    pallas_call x1, Pallas kernels, whole(): pl.pallas_call(functools.partial(whole_kernel, D, M, sizes, xchunks, rows...  108 us
    pallas_call x1, Pallas kernels, pick(): pl.pallas_call(functools.partial(pick_kernel, per, vocab_rows), name='pic...  3.37 us
    unnamed x2, local copies, waits for them, and re-layouts  2.97 us

profile of v1, /device:TPU:0, one launch (start us, length us, event | category | flops | bytes accessed | tf_op | source)
XLA Modules:
  0.0 117.2 jit_solution(4168020425201584828)
XLA Ops:
  0.6 3.4 %pick.1.contrib_ref = f32[8,1,2048]{2,1,0:T(1,128)} custom-call(s32[8]{0:T(128)} %clean_ref.1, s32[8]{0:T(128)} %corrupt_ref.1, bf16[8016,2048]{1,0:T(8,128)(2,1)} %refs_15_.1, bf16[8016,2048]{1,0:T(8,128)(2,1)} %refs_15_.1, bf16[8016,2048]{1,0:T(8,128)(2,1)} %refs_15_.1, bf16[8016,2048]{1,0:T(8,128)(2,1)} %refs_15_.1, bf16[8016,2048]{1,0:T(8,128)(2,1)} %refs_15_.1, ...), custom_call_target="tpu_custom_call" | custom-call | tf_op jit(solution)/shard_map/pick/pallas_call | solution.py:711
  4.0 108.5 %whole.1 = (bf16[256,1024]{1,0:T(8,128)(2,1)}, f32[1,8]{1,0:T(1,128)}, f32[1,1]{1,0:T(1,128)}) custom-call(bf16[256,2048]{1,0:T(8,128)(2,1)} %tok_ref.1, bf16[8192]{0:T(1024)(128)(2,1)} %gain_ref.1, bf16[1024,1024]{1,0:T(8,128)(2,1)} %wq_ref.1, bf16[1024,128]{1,0:T(8,128)(2,1)} %wk_ref.1, bf16[1024,128]{1,0:T(8,128)(2,1)} %wv_ref.1, ...), custom_call_target="tpu_custom_call" | custom-call | tf_op jit(solution)/shard_map/whole/pallas_call | solution.py:648
  112.5 1.9 %copy.18 = bf16[256,1024]{1,0:T(8,128)(2,1)} copy(bf16[256,1024]{1,0:T(8,128)(2,1)} %get-tuple-element.12) | data formatting | bytes 1048576
  114.3 1.1 copy.19

commit v2 on v1

--- a/solution.py
+++ b/solution.py
@@ -14,6 +14,7 @@
 MESH = pl.DeviceIdType.MESH
 F32 = jnp.float32
 BF16 = jnp.bfloat16
+GROUP = 16
 
 
 def flip(index, mask):
@@ -77,19 +78,24 @@
 
 
 def whole_kernel(
-    D, M, sizes, xchunks, token_count,
-    tok_ref, gain_ref, wq_ref, wk_ref, wv_ref, cos_hbm, sin_hbm, wout_hbm, contrib_ref, fgain_ref,
-    head_ref, scores_ref, metric_ref,
-    *scratch,
+    D, M, sizes, xchunks, token_count, vocab,
+    tok_ref, gain_ref, wq_ref, wk_ref, wv_ref, cos_hbm, sin_hbm, wout_hbm, fgain_ref, *rest,
 ):
+    if vocab:
+        unembed_ref, clean_ref, corrupt_ref = rest[:3]
+        head_ref, scores_ref, metric_ref, contrib_ref, slab_a, slab_b, slab_sem = rest[3:10]
+        scratch = rest[10:]
+    else:
+        contrib_ref, head_ref, scores_ref, metric_ref = rest[:4]
+        scratch = rest[4:]
     G_ = len(sizes) + 1
     w_bufs = scratch[:G_]
     (
         x_all, x_n, acc, gain_s, ss, cos_ref, sin_ref, wout_ref, tail_tok, q_s, k_s, v_s,
-        dir_all, g_src, g_all, qp_src, qp_all, pre_w, pre_t, last_src, last_all, rows_a,
+        dir_all, g_src, g_all, t_src, t_all, qp_src, qp_all, pre_w, pre_t, last_src, last_all, rows_a,
         out_src, out_all, hg_src, hg_all, tot_src, tot_all,
         loc_sem, one_sem, xs_sem, xr_sem, ps_sem, pr_sem, cs_sem, cr_sem,
-        s1, r1, s2, r2, s3, r3, s4, r4, s6, r6, s7, r7, s8, r8,
+        s1, r1, s2, r2, s3, r3, s4, r4, s6, r6, s7, r7, s8, r8, s9, r9,
     ) = scratch[G_:]
     d = lax.axis_index("dp")
     m = lax.axis_index("mp")
@@ -162,9 +168,15 @@
         early.append(pltpu.make_async_copy(
             tok_ref.at[pl.ds((b + 1) * L - 16, 16), :], tail_tok.at[b], one_sem.at[4 + b]
         ))
+    for cp in early[3:] + early[:3]:
+        cp.start()
     xown.start()
-    for cp in early:
-        cp.start()
+    for cp in early[3:]:
+        cp.wait()
+    toks = [tail_tok[b].astype(F32)[15:16, :] for b in range(S)]
+    tok = toks[0] if S == 1 else jnp.concatenate(toks, axis=0)
+    for jj in range(R):
+        t_src[jj] = tok[:, jj * cols:(jj + 1) * cols]
     for k in range(M):
         gain_s[k] = gain_ref[k * width:(k + 1) * width].astype(F32).reshape(1, width)
     ss[...] = jnp.zeros_like(ss)
@@ -376,37 +388,70 @@
         e = jnp.exp(logits - jnp.max(logits, axis=1, keepdims=True))
         return (e * (1.0 / jnp.sum(e, axis=1, keepdims=True))).astype(BF16)
 
+    def fan(src, dst, send_sem, recv_sem):
+        for i in range(M - 1, -1, -1):
+            k = (m + i) % M
+            for jj in range(R):
+                to = m * R + jj
+                if i == 0:
+                    remote(src.at[jj], dst.at[d], send_sem.at[jj, i], recv_sem.at[d], (to, k), to != d)
+                    local(src.at[jj], dst.at[d], recv_sem.at[d], to == d)
+                else:
+                    remote(src.at[jj], dst.at[d], send_sem.at[jj, i], recv_sem.at[d], (to, k))
+
+    slabs = []
+    if vocab:
+        size = -(-vocab // (4 * GROUP)) * GROUP
+        for k, lo in enumerate(range(0, vocab, size)):
+            n = min(size, vocab - lo)
+            buf = (slab_a, slab_b)[k % 2]
+            slabs.append((lo, n, buf, pltpu.make_async_copy(
+                unembed_ref.at[pl.ds(lo // GROUP, n // GROUP)], buf.at[pl.ds(0, n // GROUP)],
+                slab_sem.at[k],
+            )))
+    where = lax.broadcasted_iota(jnp.int32, (GROUP, 1), 0)
+
+    def pick_rows(k):
+        lo, n, buf, cp = slabs[k]
+        cp.wait()
+        for i in range(DS):
+            picked = []
+            for ids in (clean_ref, corrupt_ref):
+                at = ids[i] - (d * vocab + lo)
+                block = lax.div(jnp.minimum(jnp.maximum(at, 0), n - 1), GROUP)
+                got = buf[block].astype(F32)
+                hit = where == at - block * GROUP
+                picked.append(jnp.sum(jnp.where(hit, got, 0.0), axis=0, keepdims=True))
+            row = slice(i % S, i % S + 1)
+            if k == 0:
+                contrib_ref[i // S, row, :] = picked[0] - picked[1]
+            else:
+                contrib_ref[i // S, row, :] += picked[0] - picked[1]
+        if k + 2 < len(slabs):
+            slabs[k + 2][3].start()
+
+    def send_rows():
+        spread(contrib_ref, dir_all, s2, r2)
+
     def first_exchange():
-        for cp in early:
-            cp.wait()
         arrive(dir_all, r2, D)
         direction = dir_all[0]
         for j in range(1, D):
             direction = direction + dir_all[j]
         weighted = fgain_ref[...].astype(F32).reshape(1, width) * direction
-        toks = [tail_tok[b].astype(F32)[15:16, :] for b in range(S)]
-        tok = toks[0] if S == 1 else jnp.concatenate(toks, axis=0)
         for jj in range(R):
-            g_src[jj, 0:S, :] = weighted[:, jj * cols:(jj + 1) * cols]
-            g_src[jj, S:2 * S, :] = tok[:, jj * cols:(jj + 1) * cols]
-        for i in range(M - 1, -1, -1):
-            k = (m + i) % M
-            for jj in range(R):
-                to = m * R + jj
-                if i == 0:
-                    remote(g_src.at[jj], g_all.at[d], s6.at[jj, i], r6.at[d], (to, k), to != d)
-                    local(g_src.at[jj], g_all.at[d], r6.at[d], to == d)
-                else:
-                    remote(g_src.at[jj], g_all.at[d], s6.at[jj, i], r6.at[d], (to, k))
-
-    def stacked(which):
-        got = [g_all[j][which * S:(which + 1) * S, :] for j in range(D)]
-        return jnp.concatenate(got, axis=0)
+            g_src[jj] = weighted[:, jj * cols:(jj + 1) * cols]
+        fan(g_src, g_all, s6, r6)
+
+    def joined(buf):
+        return jnp.concatenate([buf[j] for j in range(D)], axis=0)
 
     def last_queries():
-        arrive(g_all, r6, D)
+        for cp in early[:3]:
+            cp.wait()
+        arrive(t_all, r9, D)
         block = pl.ds(pl.multiple_of((d % R) * cols, cols), cols)
-        lhs = (stacked(1) * gain_s[home, :, block]).astype(BF16)
+        lhs = (joined(t_all) * gain_s[home, :, block]).astype(BF16)
         mine = pl.ds((d % R) * depth, depth)
         for g in range(1, ngroups):
             lo, n = spans[g]
@@ -423,10 +468,11 @@
         )
 
     def early_grads():
-        exact = stacked(0)
+        arrive(g_all, r6, D)
+        exact = joined(g_all)
         coarse = exact.astype(BF16)
         fine = (exact - coarse.astype(F32)).astype(BF16)
-        pre = turned_back(jnp.concatenate([coarse, fine, stacked(1).astype(BF16)], axis=0))
+        pre = turned_back(jnp.concatenate([coarse, fine, joined(t_all).astype(BF16)], axis=0))
         pre_w[...] = pre[:DS] + pre[DS:2 * DS]
         pre_t[...] = pre[2 * DS:]
 
@@ -479,9 +525,9 @@
         for k in range(1, M):
             total = total + out_all[k]
         attn = total.astype(BF16)
-        residual = stacked(1) + attn.astype(F32)
+        residual = joined(t_all) + attn.astype(F32)
         sq = jnp.sum(residual * residual, axis=1, keepdims=True)
-        prod = jnp.sum(residual * stacked(0), axis=1, keepdims=True)
+        prod = jnp.sum(residual * joined(g_all), axis=1, keepdims=True)
         back = turned_back(attn) + pre_t[...]
         entries = back.shape[1]
         sq = jnp.broadcast_to(sq, (DS, entries))
@@ -572,10 +618,15 @@
                 fn = functools.partial(lambda g, r: unit(flip(m, r), g, evens), g, r)
             tasks["unit", g, r] = (deps, cost, 1 if g == 0 else 4, fn)
             unit_names[g].append((("unit", g, r), 0.0))
-    tasks["kv"] = (unit_names[0] + [("inv", 0.0)], 1.0, 1, keys_values)
-    tasks["E2"] = ([("start", 5.0)], 0.5, 2, first_exchange)
-    tasks["E3"] = ([("E2", 26.0)], 1.0, 2, last_queries)
-    tasks["pre"] = ([("E3", 0.0)], 1.0, 5, early_grads)
+    tasks["kv"] = (unit_names[0] + [("inv", 0.0), ("E3", 0.0)], 1.0, 1, keys_values)
+    before = "start"
+    for k in range(len(slabs)):
+        tasks["pick", k] = ([(before, 4.0)], 1.2, 2, functools.partial(pick_rows, k))
+        before = ("pick", k)
+    tasks["E1"] = ([(before, 0.0)], 0.1, 2, send_rows)
+    tasks["E2"] = ([("E1", 22.0)], 0.5, 2, first_exchange)
+    tasks["E3"] = ([("start", 6.0)], 1.0, 2, last_queries)
+    tasks["pre"] = ([("E2", 25.0)], 1.0, 5, early_grads)
     tasks["last"] = ([("kv", 0.0), ("E3", 20.0)], 1.5, 1, last_position)
     tasks["T1"] = ([("last", 8.0)], 1.0, 1, project_out)
     tasks["T2"] = ([("T1", 4.0), ("pre", 0.0)], 1.5, 1, residual_grads)
@@ -585,12 +636,14 @@
     tasks["tot"] = ([(("att", h), 0.0) for h in range(heads)], 0.1, 7, totals)
     tasks["fin"] = ([("tot", 0.0), ("T2", 0.0)], 0.1, 8, finish)
 
-    spread(contrib_ref, dir_all, s2, r2)
+    fan(t_src, t_all, s9, r9)
     for c in range(xchunks):
         xstart(0, c)
     own_sends(0)
     if ngroups > 1:
         own_sends(1)
+    for slab in slabs[:2]:
+        slab[3].start()
     ordered = order_tasks(events, tasks)
     timed += [(when, 2, len(timed) + i, fn) for i, (when, fn) in enumerate(ordered)]
     for _, _, _, fn in sorted(timed, key=lambda t: t[:3]):
@@ -619,7 +672,7 @@
     return cos, np.concatenate([-s, s], axis=1).astype(np.float32)
 
 
-def whole(D, M, tokens, gain, wq, wk, wv, w_out, contrib, final_gain):
+def whole(D, M, tokens, gain, wq, wk, wv, w_out, final_gain, unembed, clean_ids, corrupt_ids):
     rows, width = tokens.shape
     S = rows // SEQUENCE_LENGTH
     depth = wq.shape[0]
@@ -645,22 +698,33 @@
     def h(*shape):
         return pltpu.VMEM(shape, BF16)
 
+    I = pl.BlockSpec(memory_space=pltpu.SMEM)
+    vocab = unembed.shape[0] if unembed.shape[0] % GROUP == 0 else 0
+    if vocab:
+        slab = -(-vocab // (4 * GROUP)) * GROUP
+        blocks = unembed.reshape(vocab // GROUP, GROUP, width)
+        source, source_specs = (blocks, clean_ids, corrupt_ids), [ANY, I, I]
+        pages = [h(slab // GROUP, GROUP, width)] * 2
+        source_scratch = [f(D, S, width)] + pages + [DMA((4,))]
+    else:
+        source = (pick(unembed, clean_ids, corrupt_ids).reshape(D, S, width),)
+        source_specs, source_scratch = [V], []
     return pl.pallas_call(
-        functools.partial(whole_kernel, D, M, sizes, xchunks, rows * D),
+        functools.partial(whole_kernel, D, M, sizes, xchunks, rows * D, vocab),
         name="whole",
         out_shape=[
             jax.ShapeDtypeStruct((rows, entries), BF16),
             jax.ShapeDtypeStruct((S, heads), F32),
             jax.ShapeDtypeStruct((S, 1), F32),
         ],
-        in_specs=[ANY, V, ANY, ANY, ANY, ANY, ANY, ANY, V, V],
+        in_specs=[ANY, V, ANY, ANY, ANY, ANY, ANY, ANY, V] + source_specs,
         out_specs=[V, V, V],
-        scratch_shapes=[h(M, width, n) for n in [kvw] + [k * HEAD_SIZE for k in sizes]] + [
+        scratch_shapes=source_scratch + [h(M, width, n) for n in [kvw] + [k * HEAD_SIZE for k in sizes]] + [
             h(M, rows, width), h(M, rows, width), f(rows, total), f(M, 1, width), f(rows, 1),
             f(SEQUENCE_LENGTH, HEAD_SIZE), f(SEQUENCE_LENGTH, HEAD_SIZE),
             h(entries, cols), h(S, 16, width), f(heads // kv_heads, HEAD_SIZE),
             h(S * kv_heads, SEQUENCE_LENGTH, HEAD_SIZE), h(S * kv_heads, SEQUENCE_LENGTH, HEAD_SIZE),
-            f(D, S, width), f(R, 2 * S, cols), f(D, 2 * S, cols),
+            f(D, S, width), f(R, S, cols), f(D, S, cols), f(R, S, cols), f(D, S, cols),
             f(D, S, entries), f(D, S, entries), f(D * S, entries), f(D * S, entries),
             f(S, entries), f(D, S, entries), f(D * S, entries),
             f(D * S, cols), f(M, D * S, cols), f(D, 4 * S, entries), f(D, 4 * S, entries),
@@ -670,16 +734,13 @@
             DMA((parts, half, ngroups, steps)), DMA((parts, half, ngroups)),
             DMA((parts, half, ngroups)), DMA((parts, half, ngroups)),
             DMA((D,)), DMA((D,)), DMA((D,)), DMA((D,)), DMA((M,)), DMA((M,)), DMA((D,)), DMA((D,)),
-            DMA((R, M)), DMA((D,)), DMA((D,)), DMA((D,)), DMA((D,)), DMA((D,)),
+            DMA((R, M)), DMA((D,)), DMA((D,)), DMA((D,)), DMA((D,)), DMA((D,)), DMA((R, M)), DMA((D,)),
         ],
         compiler_params=pltpu.CompilerParams(
             collective_id=0, has_side_effects=True, vmem_limit_bytes=56 * 1024 * 1024
         ),
-    )(tokens, gain, wq, wk, wv, jnp.asarray(cos), jnp.asarray(sin), w_out, contrib,
-      final_gain)
-
-
-GROUP = 16
+    )(tokens, gain, wq, wk, wv, jnp.asarray(cos), jnp.asarray(sin), w_out,
+      final_gain, *source)
 
 
 def pick_kernel(per, vocab_rows, clean_ref, corrupt_ref, *refs):
@@ -726,10 +787,9 @@
     clean_ids, corrupt_ids,
 ):
     S = tokens.shape[0] // SEQUENCE_LENGTH
-    width = unembed.shape[1]
-    contrib = pick(unembed, clean_ids, corrupt_ids).reshape(D, S, width)
     head_out, scores, metric = whole(
-        D, M, tokens, attn_gain, w_query, key_w, value_w, w_out, contrib, final_gain
+        D, M, tokens, attn_gain, w_query, key_w, value_w, w_out, final_gain, unembed,
+        clean_ids, corrupt_ids,
     )
     return head_out, scores, metric.reshape(S)
 

time: 118 us -> 115 us (0.975)
  Pallas kernels: 112 us -> 109 us
    pallas_call x1 -> x0, Pallas kernels: 3.37 us -> none  [pick(): pl.pallas_call(functools.partial(pick_kernel, per, vocab_rows), name='pic...]
where the time goes in v2:
time: 115 us
  Pallas kernels  109 us (95%)
  local copies, waits for them, and re-layouts  2.97 us (3%)
  between operations  2.41 us (2%)
    pallas_call x1, Pallas kernels, whole(): pl.pallas_call(functools.partial(whole_kernel, D, M, sizes, xchunks, rows...  109 us
    unnamed x2, local copies, waits for them, and re-layouts  2.97 us

profile of v2, /device:TPU:0, one launch (start us, length us, event | category | flops | bytes accessed | tf_op | source)
XLA Modules:
  0.0 114.6 jit_solution(11687946166641668720)
XLA Ops:
  0.6 109.2 %whole.1 = (bf16[256,1024]{1,0:T(8,128)(2,1)}, f32[1,8]{1,0:T(1,128)}, f32[1,1]{1,0:T(1,128)}) custom-call(bf16[256,2048]{1,0:T(8,128)(2,1)} %tok_ref.1, bf16[8192]{0:T(1024)(128)(2,1)} %gain_ref.1, bf16[1024,1024]{1,0:T(8,128)(2,1)} %wq_ref.1, bf16[1024,128]{1,0:T(8,128)(2,1)} %wk_ref.1, bf16[1024,128]{1,0:T(8,128)(2,1)} %wv_ref.1, ...), custom_call_target="tpu_custom_call" | custom-call | tf_op jit(solution)/shard_map/whole/pallas_call | solution.py:712
  109.9 1.9 %copy.18 = bf16[256,1024]{1,0:T(8,128)(2,1)} copy(bf16[256,1024]{1,0:T(8,128)(2,1)} %get-tuple-element.12) | data formatting | bytes 1048576
  111.7 1.1 copy.19

commit v3 on v2

--- a/solution.py
+++ b/solution.py
@@ -50,7 +50,7 @@
 def head_groups(heads, piece):
     if piece < 256 or heads < 4:
         return [heads]
-    sizes = [2] * ((heads - 2) // 2)
+    sizes = [2] * ((heads - 4) // 2)
     return sizes + [1] * (heads - sum(sizes))
 
 
@@ -268,15 +268,13 @@
         for cp in own.pop((g, p), []):
             cp.wait()
 
-    def own_sends(g):
+    def own_send(g, step):
         for p in range(parts):
             own_ready(g, p)
-            wsend(0, g, p, 0)
-        for step in range(1, steps):
+            wsend(0, g, p, step)
+        if step == steps - 1:
             for p in range(parts):
-                wsend(0, g, p, step)
-        for p in range(parts):
-            csend(0, g, p)
+                csend(0, g, p)
 
     pace = 46e3
     hops = len(plan[0][0])
@@ -286,11 +284,9 @@
     share = hops / rounds
     own_at, rel_at = {}, {}
     clock = 0.0
-    queue = [("own", 0)] + ([("own", 1)] if ngroups > 1 else [])
+    queue = []
     for g in range(ngroups):
-        queue.append(("rel", g))
-        if g + 2 < ngroups:
-            queue.append(("own", g + 2))
+        queue += [("own", g), ("rel", g)]
     for kind, g in queue:
         if kind == "own":
             own_at[g] = clock
@@ -317,8 +313,6 @@
                     for later in range(step + 1, steps):
                         wsend(mask, g, p, later)
                     csend(mask, g, p)
-                if i == 0 and g + 2 < ngroups:
-                    own_sends(g + 2)
 
             timed.append((when, 0, len(timed), arrival))
             events["w", g, i] = when
@@ -639,9 +633,12 @@
     fan(t_src, t_all, s9, r9)
     for c in range(xchunks):
         xstart(0, c)
-    own_sends(0)
-    if ngroups > 1:
-        own_sends(1)
+    for step in range(steps):
+        own_send(0, step)
+    for g in range(1, ngroups):
+        for step in range(steps):
+            when = own_at[g] + group_time[g] * share * step / steps - 4.0
+            timed.append((when, -1, len(timed), functools.partial(own_send, g, step)))
     for slab in slabs[:2]:
         slab[3].start()
     ordered = order_tasks(events, tasks)
@@ -713,9 +710,9 @@
         functools.partial(whole_kernel, D, M, sizes, xchunks, rows * D, vocab),
         name="whole",
         out_shape=[
-            jax.ShapeDtypeStruct((rows, entries), BF16),
-            jax.ShapeDtypeStruct((S, heads), F32),
-            jax.ShapeDtypeStruct((S, 1), F32),
+            pltpu.VMEM((rows, entries), BF16),
+            pltpu.VMEM((S, heads), F32),
+            pltpu.VMEM((S, 1), F32),
         ],
         in_specs=[ANY, V, ANY, ANY, ANY, ANY, ANY, ANY, V] + source_specs,
         out_specs=[V, V, V],
@@ -782,6 +779,32 @@
     )(clean_ids, corrupt_ids, *([unembed] * (2 * per)))
 
 
+def settle_kernel(head_ref, scores_ref, metric_ref, head_out, scores_out, metric_out, sem):
+    moves = [
+        pltpu.make_async_copy(src, dst, sem.at[i])
+        for i, (src, dst) in enumerate(
+            ((head_ref, head_out), (scores_ref, scores_out), (metric_ref, metric_out))
+        )
+    ]
+    for cp in moves:
+        cp.start()
+    for cp in moves:
+        cp.wait()
+
+
+def settle(head, scores, metric):
+    V = pl.BlockSpec(memory_space=pltpu.VMEM)
+    ANY = pl.BlockSpec(memory_space=pl.ANY)
+    return pl.pallas_call(
+        settle_kernel,
+        name="settle",
+        out_shape=[jax.ShapeDtypeStruct(x.shape, x.dtype) for x in (head, scores, metric)],
+        in_specs=[ANY, ANY, ANY],
+        out_specs=[ANY, ANY, ANY],
+        scratch_shapes=[pltpu.SemaphoreType.DMA((3,))],
+    )(*(pltpu.with_memory_space_constraint(x, pltpu.VMEM) for x in (head, scores, metric)))
+
+
 def per_device(
     D, M, tokens, attn_gain, w_query, key_w, value_w, w_out, final_gain, unembed,
     clean_ids, corrupt_ids,
@@ -791,6 +814,7 @@
         D, M, tokens, attn_gain, w_query, key_w, value_w, w_out, final_gain, unembed,
         clean_ids, corrupt_ids,
     )
+    head_out, scores, metric = settle(head_out, scores, metric)
     return head_out, scores, metric.reshape(S)
 
 

time: 115 us -> 109 us (0.948)
  local copies, waits for them, and re-layouts: 2.97 us -> 0 us
  between operations: 2.41 us -> 0.8 us
    unnamed x2 -> x0, local copies, waits for them, and re-layouts: 2.97 us -> none
    pallas_call x1, Pallas kernels: 109 us -> 107 us  [whole(): pl.pallas_call(functools.partial(whole_kernel, D, M, sizes, xchunks, rows...]
    pallas_call x0 -> x1, Pallas kernels: none -> 1.46 us  [settle(): pl.pallas_call(settle_kernel, name='settle', out_shape=[jax.ShapeDtypeStr...]
where the time goes in v3:
time: 109 us
  Pallas kernels  108 us (99%)
    pallas_call x1, Pallas kernels, whole(): pl.pallas_call(functools.partial(whole_kernel, D, M, sizes, xchunks, rows...  107 us

profile of v3, /device:TPU:0, one launch (start us, length us, event | category | flops | bytes accessed | tf_op | source)
XLA Modules:
  0.0 109.2 jit_solution(400416758690194953)
XLA Ops:
  0.6 107.0 %whole.1 = (bf16[256,1024]{1,0:T(8,128)(2,1)S(1)}, f32[1,8]{1,0:T(1,128)S(1)}, f32[1,1]{1,0:T(1,128)}) custom-call(bf16[256,2048]{1,0:T(8,128)(2,1)} %tok_ref.1, bf16[8192]{0:T(1024)(128)(2,1)} %gain_ref.1, bf16[1024,1024]{1,0:T(8,128)(2,1)} %wq_ref.1, bf16[1024,128]{1,0:T(8,128)(2,1)} %wk_ref.1, bf16[1024,128]{1,0:T(8,128)(2,1)} %wv_ref.1, ...), custom_call_target="tpu_custom_call" | custom-call | tf_op jit(solution)/shard_map/whole/pallas_call | solution.py:709
  107.6 1.5 %settle.1 = (bf16[256,1024]{1,0:T(8,128)(2,1)}, f32[1,8]{1,0:T(1,128)}, f32[1,1]{1,0:T(1,128)}) custom-call(bf16[256,1024]{1,0:T(8,128)(2,1)S(1)} %get-tuple-element.9.head_ref, f32[1,8]{1,0:T(1,128)S(1)} %get-tuple-element.10.scores_ref, f32[1,1]{1,0:T(1,128)} %get-tuple-element.11.metric_ref), custom_call_target="tpu_custom_call" | custom-call | tf_op jit(solution)/shard_map/settle/pallas_call | solution.py:798

commit v4 on v3

--- a/solution.py
+++ b/solution.py
@@ -91,10 +91,10 @@
     G_ = len(sizes) + 1
     w_bufs = scratch[:G_]
     (
-        x_all, x_n, acc, gain_s, ss, cos_ref, sin_ref, wout_ref, tail_tok, q_s, k_s, v_s,
+        x_all, x_n, acc, gain_s, gain_v, fgain_v, ss, cos_ref, sin_ref, wout_ref, tail_tok, q_s, k_s, v_s,
         dir_all, g_src, g_all, t_src, t_all, qp_src, qp_all, pre_w, pre_t, last_src, last_all, rows_a,
         out_src, out_all, hg_src, hg_all, tot_src, tot_all,
-        loc_sem, one_sem, xs_sem, xr_sem, ps_sem, pr_sem, cs_sem, cr_sem,
+        far_sem, loc_sem, one_sem, xs_sem, xr_sem, ps_sem, pr_sem, cs_sem, cr_sem,
         s1, r1, s2, r2, s3, r3, s4, r4, s6, r6, s7, r7, s8, r8, s9, r9,
     ) = scratch[G_:]
     d = lax.axis_index("dp")
@@ -132,6 +132,24 @@
     def wref(owner, g, p):
         return w_bufs[g].at[owner // R, pl.ds((owner % R) * depth + p * piece, piece), :]
 
+    barrier = pltpu.get_barrier_semaphore()
+
+    bits = []
+    while 2 ** len(bits) < D:
+        bits.append(2 ** len(bits))
+
+    def tell(sem):
+        for near, ok in ((m - 1, m > 0), (m + 1, m < M - 1)):
+            @pl.when(ok)
+            def _(near=near):
+                pl.semaphore_signal(sem, inc=1, device_id=(d, near), device_id_type=MESH)
+
+    beside = jnp.minimum(m, 1) + jnp.minimum(M - 1 - m, 1)
+
+    for bit in bits:
+        pl.semaphore_signal(barrier, inc=1, device_id=(flip(d, bit), m), device_id_type=MESH)
+    tell(barrier)
+
     own = {}
     for g in range(ngroups):
         for p in range(parts):
@@ -149,15 +167,6 @@
             for cp in own[g, p]:
                 cp.start()
 
-    barrier = pltpu.get_barrier_semaphore()
-
-    @pl.loop(1, everyone)
-    def _(i):
-        other = (me + i) % everyone
-        pl.semaphore_signal(
-            barrier, inc=1, device_id=(other // M, other % M), device_id_type=MESH
-        )
-
     xown = pltpu.make_async_copy(tok_ref, x_all.at[m], one_sem.at[0])
     early = [
         pltpu.make_async_copy(cos_hbm, cos_ref, one_sem.at[1]),
@@ -168,21 +177,26 @@
         early.append(pltpu.make_async_copy(
             tok_ref.at[pl.ds((b + 1) * L - 16, 16), :], tail_tok.at[b], one_sem.at[4 + b]
         ))
-    for cp in early[3:] + early[:3]:
+    gains_in = [
+        pltpu.make_async_copy(gain_ref, gain_v, one_sem.at[4 + S]),
+        pltpu.make_async_copy(fgain_ref, fgain_v, one_sem.at[5 + S]),
+    ]
+    for cp in early[3:] + gains_in + early[:3]:
         cp.start()
     xown.start()
-    for cp in early[3:]:
-        cp.wait()
-    toks = [tail_tok[b].astype(F32)[15:16, :] for b in range(S)]
-    tok = toks[0] if S == 1 else jnp.concatenate(toks, axis=0)
-    for jj in range(R):
-        t_src[jj] = tok[:, jj * cols:(jj + 1) * cols]
-    for k in range(M):
-        gain_s[k] = gain_ref[k * width:(k + 1) * width].astype(F32).reshape(1, width)
     ss[...] = jnp.zeros_like(ss)
-    pl.semaphore_wait(barrier, everyone - 1)
+    pl.semaphore_wait(barrier, len(bits) + beside)
 
     pending = []
+    stamp = [0.0]
+
+    def settle_sends(before):
+        while pending and pending[0][0] < before:
+            _, cp, cond = pending.pop(0)
+            if cond is None:
+                cp.wait_send()
+            else:
+                pl.when(cond)(cp.wait_send)
 
     def remote(src, dst, send_sem, recv_sem, to, cond=None):
         cp = pltpu.make_async_remote_copy(
@@ -193,7 +207,7 @@
             cp.start()
         else:
             pl.when(cond)(cp.start)
-        pending.append((cp, cond))
+        pending.append((stamp[0], cp, cond))
 
     def local(src, dst, sem, cond=None):
         cp = pltpu.make_async_copy(src, dst, sem)
@@ -232,9 +246,9 @@
 
     def xstart(hop, c):
         for side in range(2):
-            @pl.when(xpred(hop, side))
-            def _(side=side):
-                xsend(hop, c, side).start()
+            cp = xsend(hop, c, side)
+            pl.when(xpred(hop, side))(cp.start)
+            pending.append((stamp[0], cp, xpred(hop, side)))
 
     def xwait(hop, c):
         rr = pl.ds(c * xpiece, xpiece)
@@ -432,7 +446,7 @@
         direction = dir_all[0]
         for j in range(1, D):
             direction = direction + dir_all[j]
-        weighted = fgain_ref[...].astype(F32).reshape(1, width) * direction
+        weighted = fgain_v[...].astype(F32).reshape(1, width) * direction
         for jj in range(R):
             g_src[jj] = weighted[:, jj * cols:(jj + 1) * cols]
         fan(g_src, g_all, s6, r6)
@@ -619,7 +633,7 @@
         before = ("pick", k)
     tasks["E1"] = ([(before, 0.0)], 0.1, 2, send_rows)
     tasks["E2"] = ([("E1", 22.0)], 0.5, 2, first_exchange)
-    tasks["E3"] = ([("start", 6.0)], 1.0, 2, last_queries)
+    tasks["E3"] = ([("start", 17.0)], 1.0, 2, last_queries)
     tasks["pre"] = ([("E2", 25.0)], 1.0, 5, early_grads)
     tasks["last"] = ([("kv", 0.0), ("E3", 20.0)], 1.5, 1, last_position)
     tasks["T1"] = ([("last", 8.0)], 1.0, 1, project_out)
@@ -630,11 +644,26 @@
     tasks["tot"] = ([(("att", h), 0.0) for h in range(heads)], 0.1, 7, totals)
     tasks["fin"] = ([("tot", 0.0), ("T2", 0.0)], 0.1, 8, finish)
 
-    fan(t_src, t_all, s9, r9)
-    for c in range(xchunks):
-        xstart(0, c)
     for step in range(steps):
         own_send(0, step)
+    xstart(0, 0)
+    for i, bit in enumerate(bits):
+        pl.semaphore_signal(far_sem.at[i], inc=1, device_id=(flip(d, bit), m), device_id_type=MESH)
+        pl.semaphore_wait(far_sem.at[i], 1)
+    for i in range(len(bits), len(bits) + M - 1):
+        tell(far_sem.at[i])
+        pl.semaphore_wait(far_sem.at[i], beside)
+    for cp in early[3:] + gains_in:
+        cp.wait()
+    toks = [tail_tok[b].astype(F32)[15:16, :] for b in range(S)]
+    tok = toks[0] if S == 1 else jnp.concatenate(toks, axis=0)
+    for jj in range(R):
+        t_src[jj] = tok[:, jj * cols:(jj + 1) * cols]
+    fan(t_src, t_all, s9, r9)
+    for c in range(1, xchunks):
+        xstart(0, c)
+    for k in range(M):
+        gain_s[k] = gain_v[k * width:(k + 1) * width].astype(F32).reshape(1, width)
     for g in range(1, ngroups):
         for step in range(steps):
             when = own_at[g] + group_time[g] * share * step / steps - 4.0
@@ -643,21 +672,13 @@
         slab[3].start()
     ordered = order_tasks(events, tasks)
     timed += [(when, 2, len(timed) + i, fn) for i, (when, fn) in enumerate(ordered)]
-    for _, _, _, fn in sorted(timed, key=lambda t: t[:3]):
+    for when, _, _, fn in sorted(timed, key=lambda t: t[:3]):
+        stamp[0] = when
+        settle_sends(when - 20.0)
         fn()
     for g in range(ngroups):
         partner(g, evens)
-    for h in range(M - 1):
-        for c in range(xchunks):
-            for side in range(2):
-                @pl.when(xpred(h, side))
-                def _(h=h, c=c, side=side):
-                    xsend(h, c, side).wait_send()
-    for cp, cond in pending:
-        if cond is None:
-            cp.wait_send()
-        else:
-            pl.when(cond)(cp.wait_send)
+    settle_sends(math.inf)
 
 
 def tables():
@@ -714,10 +735,10 @@
             pltpu.VMEM((S, heads), F32),
             pltpu.VMEM((S, 1), F32),
         ],
-        in_specs=[ANY, V, ANY, ANY, ANY, ANY, ANY, ANY, V] + source_specs,
+        in_specs=[ANY] * 9 + source_specs,
         out_specs=[V, V, V],
         scratch_shapes=source_scratch + [h(M, width, n) for n in [kvw] + [k * HEAD_SIZE for k in sizes]] + [
-            h(M, rows, width), h(M, rows, width), f(rows, total), f(M, 1, width), f(rows, 1),
+            h(M, rows, width), h(M, rows, width), f(rows, total), f(M, 1, width), h(M * width), h(width), f(rows, 1),
             f(SEQUENCE_LENGTH, HEAD_SIZE), f(SEQUENCE_LENGTH, HEAD_SIZE),
             h(entries, cols), h(S, 16, width), f(heads // kv_heads, HEAD_SIZE),
             h(S * kv_heads, SEQUENCE_LENGTH, HEAD_SIZE), h(S * kv_heads, SEQUENCE_LENGTH, HEAD_SIZE),
@@ -726,7 +747,7 @@
             f(S, entries), f(D, S, entries), f(D * S, entries),
             f(D * S, cols), f(M, D * S, cols), f(D, 4 * S, entries), f(D, 4 * S, entries),
             f(1, entries), f(D, 1, entries),
-            DMA((ngroups, parts, 2)), DMA((4 + S,)),
+            pltpu.SemaphoreType.REGULAR((D.bit_length() + M,)), DMA((ngroups, parts, 2)), DMA((6 + S,)),
             DMA((M - 1, xchunks, 2)), DMA((M - 1, xchunks, 2)),
             DMA((parts, half, ngroups, steps)), DMA((parts, half, ngroups)),
             DMA((parts, half, ngroups)), DMA((parts, half, ngroups)),

time: 109 us -> 106 us (0.972)
  Pallas kernels: 108 us -> 105 us
    pallas_call x1, Pallas kernels: 107 us -> 104 us  [whole(): pl.pallas_call(functools.partial(whole_kernel, D, M, sizes, xchunks, rows...]
where the time goes in v4:
time: 106 us
  Pallas kernels  105 us (99%)
    pallas_call x1, Pallas kernels, whole(): pl.pallas_call(functools.partial(whole_kernel, D, M, sizes, xchunks, rows...  104 us

profile of v4, /device:TPU:0, one launch (start us, length us, event | category | flops | bytes accessed | tf_op | source)
XLA Modules:
  0.0 106.1 jit_solution(10518295677741897370)
XLA Ops:
  0.6 103.9 %whole.1 = (bf16[256,1024]{1,0:T(8,128)(2,1)S(1)}, f32[1,8]{1,0:T(1,128)S(1)}, f32[1,1]{1,0:T(1,128)}) custom-call(bf16[256,2048]{1,0:T(8,128)(2,1)} %tok_ref.1, bf16[8192]{0:T(1024)(128)(2,1)} %gain_ref.1, bf16[1024,1024]{1,0:T(8,128)(2,1)} %wq_ref.1, bf16[1024,128]{1,0:T(8,128)(2,1)} %wk_ref.1, bf16[1024,128]{1,0:T(8,128)(2,1)} %wv_ref.1, ...), custom_call_target="tpu_custom_call" | custom-call | tf_op jit(solution)/shard_map/whole/pallas_call | solution.py:730
  104.5 1.5 %settle.1 = (bf16[256,1024]{1,0:T(8,128)(2,1)}, f32[1,8]{1,0:T(1,128)}, f32[1,1]{1,0:T(1,128)}) custom-call(bf16[256,1024]{1,0:T(8,128)(2,1)S(1)} %get-tuple-element.9.head_ref, f32[1,8]{1,0:T(1,128)S(1)} %get-tuple-element.10.scores_ref, f32[1,1]{1,0:T(1,128)} %get-tuple-element.11.metric_ref), custom_call_target="tpu_custom_call" | custom-call | tf_op jit(solution)/shard_map/settle/pallas_call | solution.py:819

commit v5 on v4

--- a/solution.py
+++ b/solution.py
@@ -367,13 +367,13 @@
 
     evens = list(range(0, D, 2))
 
-    def gained(r):
-        if r == 0:
+    def gained(r, c):
+        if r == 0 and c == 0:
             xown.wait()
         shard = flip(m, r)
         block = 32
 
-        @pl.loop(0, rows // block)
+        @pl.loop(c * xpiece // block, (c + 1) * xpiece // block)
         def _(i):
             rr = pl.ds(pl.multiple_of(i * block, block), block)
             xv = x_all[shard, rr, :].astype(F32)
@@ -604,10 +604,15 @@
         scores_ref[...] = scores
 
     tasks = {}
+    gain_names = {}
     for r in range(M):
-        deps = [("start", 2.0)] if r == 0 else [(("x", r - 1, xchunks - 1), 0.1)]
-        tasks["gain", r] = (deps, 1.0, 0, functools.partial(gained, r))
-    gains = [(("gain", r), 0.0) for r in range(M)]
+        for c in range(xchunks):
+            deps = [("start", 2.0)] if r == 0 else [(("x", r - 1, c), 0.1)]
+            if c:
+                deps.append((("gain", r, c - 1), 0.0))
+            tasks["gain", r, c] = (deps, 1.0 / xchunks, 0, functools.partial(gained, r, c))
+        gain_names[r] = [(("gain", r, c), 0.0) for c in range(xchunks)]
+    gains = [name for r in range(M) for name in gain_names[r]]
     tasks["inv"] = (gains, 0.1, 0, inverse_rms)
     unit_names = {g: [] for g in range(ngroups)}
     for g in range(ngroups):
@@ -622,7 +627,7 @@
                 ]
                 fn = functools.partial(lambda g, r, ms: unit(flip(home, r), g, ms), g, r, masks)
             else:
-                deps = [(("gain", r), 0.0)] + [(("w", g, i), 1.6) for i in range(rounds)]
+                deps = gain_names[r] + [(("w", g, i), 1.6) for i in range(rounds)]
                 fn = functools.partial(lambda g, r: unit(flip(m, r), g, evens), g, r)
             tasks["unit", g, r] = (deps, cost, 1 if g == 0 else 4, fn)
             unit_names[g].append((("unit", g, r), 0.0))
@@ -666,7 +671,7 @@
         gain_s[k] = gain_v[k * width:(k + 1) * width].astype(F32).reshape(1, width)
     for g in range(1, ngroups):
         for step in range(steps):
-            when = own_at[g] + group_time[g] * share * step / steps - 4.0
+            when = own_at[g] + group_time[g] * share * step / steps - 3.0
             timed.append((when, -1, len(timed), functools.partial(own_send, g, step)))
     for slab in slabs[:2]:
         slab[3].start()

time: 106 us -> 106 us (level)
  no operation moved by 1% of the time
where the time goes in v5:
time: 106 us
  Pallas kernels  105 us (99%)
    pallas_call x1, Pallas kernels, whole(): pl.pallas_call(functools.partial(whole_kernel, D, M, sizes, xchunks, rows...  103 us

profile of v5, /device:TPU:0, one launch (start us, length us, event | category | flops | bytes accessed | tf_op | source)
XLA Modules:
  0.0 105.6 jit_solution(2923658367793524256)
XLA Ops:
  0.6 103.3 %whole.1 = (bf16[256,1024]{1,0:T(8,128)(2,1)S(1)}, f32[1,8]{1,0:T(1,128)S(1)}, f32[1,1]{1,0:T(1,128)}) custom-call(bf16[256,2048]{1,0:T(8,128)(2,1)} %tok_ref.1, bf16[8192]{0:T(1024)(128)(2,1)} %gain_ref.1, bf16[1024,1024]{1,0:T(8,128)(2,1)} %wq_ref.1, bf16[1024,128]{1,0:T(8,128)(2,1)} %wk_ref.1, bf16[1024,128]{1,0:T(8,128)(2,1)} %wv_ref.1, ...), custom_call_target="tpu_custom_call" | custom-call | tf_op jit(solution)/shard_map/whole/pallas_call | solution.py:735
  103.9 1.5 %settle.1 = (bf16[256,1024]{1,0:T(8,128)(2,1)}, f32[1,8]{1,0:T(1,128)}, f32[1,1]{1,0:T(1,128)}) custom-call(bf16[256,1024]{1,0:T(8,128)(2,1)S(1)} %get-tuple-element.9.head_ref, f32[1,8]{1,0:T(1,128)S(1)} %get-tuple-element.10.scores_ref, f32[1,1]{1,0:T(1,128)} %get-tuple-element.11.metric_ref), custom_call_target="tpu_custom_call" | custom-call | tf_op jit(solution)/shard_map/settle/pallas_call | solution.py:824
